TPU v7x, 768 devices: a whole 4x8x12 slice. The times are simulated.
768 devices in a mesh: ctx: 24 (over z, core), head: 32 (over x, y).
Axes of the slice: x: 4, y: 8, z: 12, core: 2. Of those that a mesh axis runs over, the one named last changes fastest.
Arguments:
- queries: bfloat16 [12288, 8192], P('ctx', 'head'), may hold values from -24 to 24, as said below
- keys: bfloat16 [12288, 1024], P('ctx'), may hold values from -24 to 24
- values: bfloat16 [12288, 1024], P('ctx'), may hold values from -6 to 6
- out_grad: bfloat16 [12288, 8192], P('ctx', 'head'), may hold values from -6 to 6
- doc_start: int32 [12288], P('ctx'), may hold values from 0 to 12287, as said below
Outputs:
- attn_out: bfloat16 [12288, 8192], P('ctx', 'head')
- query_grad: bfloat16 [12288, 8192], P('ctx', 'head')
- key_grad: float32 [12288, 1024], P('ctx', 'head')
- value_grad: float32 [12288, 1024], P('ctx', 'head')
Inputs may be any that keep to these rules, and one draw needn't show every extreme that they name: Query and key entries lie within the range; in some draws a few queries are close to multiples of visible keys. doc_start[0] = 0; for i > 0 either doc_start[i] = i (a document begins) or doc_start[i] = doc_start[i - 1]. Documents may cross device boundaries. The last token begins a document of its own.
All inputs are finite; a program needn't handle non-finite values.
Results may differ from a plain program's by a relative error of at most 0.019.
Values may be sent and summed in bfloat16 or wider, within the bound.
A program may use at most 32 MiB of HBM per device.

v0:
```python
import jax
import jax.numpy as jnp
from jax import lax
from jax.sharding import PartitionSpec as P

HEAD_DIM = 128
WINDOW = 1024


def from_behind(block, axis, distance):
    devices = range(lax.axis_size(axis))
    route = [(i - distance, i) for i in devices if i - distance in devices]
    return lax.ppermute(block, axis, route)


def from_partner(array, axis, stride):
    return lax.ppermute(array, axis, [(i, i ^ 1 << stride) for i in range(lax.axis_size(axis))])


def return_tails(grad_ext, key_reach, tok_rows, hop_count):
    owned_rows = grad_ext[:, key_reach:]
    offset = 0
    for distance in range(hop_count, 0, -1):
        row_count = min(tok_rows, key_reach - (distance - 1) * tok_rows)
        piece = grad_ext[:, offset : offset + row_count]
        offset = offset + row_count
        returned = from_behind(piece.astype(jnp.bfloat16), "ctx", -distance).astype(piece.dtype)
        owned_rows = owned_rows.at[:, tok_rows - row_count :].add(returned)
    return owned_rows


def group_sum(partial_value, head_index):
    head_width = partial_value.shape[2]
    quarter = head_width // 4
    partial_value = partial_value + from_partner(
        partial_value.astype(jnp.bfloat16), "head", 0
    ).astype(partial_value.dtype)
    partial_value = partial_value + from_partner(
        partial_value.astype(jnp.bfloat16), "head", 1
    ).astype(partial_value.dtype)
    return lax.dynamic_slice_in_dim(partial_value, head_index % 4 * quarter, quarter, 2)


def body(queries, keys, values, out_grad, doc_start):
    tok_rows = queries.shape[0]
    head_width = HEAD_DIM
    key_reach = WINDOW
    score_scale = HEAD_DIM ** (-0.5)
    head_index = lax.axis_index("head")
    kv_group = head_index // 4
    key_own = lax.dynamic_slice_in_dim(keys, kv_group * head_width, head_width, 1)
    value_own = lax.dynamic_slice_in_dim(values, kv_group * head_width, head_width, 1)
    stacked = jnp.stack([key_own, value_own])
    seq_offset = lax.axis_index("ctx") * tok_rows
    hop_count = -(-key_reach // tok_rows)
    pieces = []
    for distance in range(hop_count, 0, -1):
        pieces.append(from_behind(stacked, "ctx", distance))
    extended = jnp.concatenate(pieces + [stacked], axis=1)
    block_rows = min(512, tok_rows)
    query_heads = queries.reshape(tok_rows, 2, head_width)
    grad_heads = out_grad.reshape(tok_rows, 2, head_width)
    key_grad_ext = jnp.zeros((key_reach + tok_rows, head_width), jnp.float32)
    value_grad_ext = jnp.zeros((key_reach + tok_rows, head_width), jnp.float32)
    key_block = extended[0, 0 : block_rows + key_reach]
    value_block = extended[1, 0 : block_rows + key_reach]
    query_pos = seq_offset + 0 + jnp.arange(block_rows, dtype=jnp.int32)
    key_pos = seq_offset + 0 - key_reach + jnp.arange(block_rows + key_reach, dtype=jnp.int32)
    visible = (
        (key_pos[None, :] <= query_pos[:, None])
        & (key_pos[None, :] > query_pos[:, None] - key_reach)
        & (key_pos[None, :] >= doc_start[:, None])
    )
    scores = (
        jnp.einsum("qgd,kd->gqk", query_heads, key_block, preferred_element_type=jnp.float32)
        * score_scale
    )
    masked = jnp.where(visible[None], scores, -1e30)
    row_max = jnp.max(masked, axis=-1, keepdims=True)
    weights = jnp.where(visible[None], jnp.exp(masked - row_max), 0.0)
    prob_full = weights / jnp.sum(weights, axis=-1, keepdims=True)
    prob_round = prob_full.astype(jnp.bfloat16)
    attended = jnp.einsum(
        "gqk,kd->qgd", prob_round, value_block, preferred_element_type=jnp.float32
    ).astype(jnp.bfloat16)
    dprob = jnp.einsum("qgd,kd->gqk", grad_heads, value_block, preferred_element_type=jnp.float32)
    row_delta = jnp.transpose(
        jnp.sum(grad_heads.astype(jnp.float32) * attended.astype(jnp.float32), axis=-1), (1, 0)
    )
    dscore = (prob_full * (dprob - row_delta[:, :, None])).astype(jnp.bfloat16)
    qgrad_blocks = (
        jnp.einsum("gqk,kd->qgd", dscore, key_block, preferred_element_type=jnp.float32)
        * score_scale
    ).astype(jnp.bfloat16)
    key_part = (
        jnp.einsum("gqk,qgd->kd", dscore, query_heads, preferred_element_type=jnp.float32)
        * score_scale
    )
    value_part = jnp.einsum(
        "gqk,qgd->kd", prob_round, grad_heads, preferred_element_type=jnp.float32
    )
    key_grad_ext = key_grad_ext.at[0 : block_rows + key_reach].add(key_part)
    value_grad_ext = value_grad_ext.at[0 : block_rows + key_reach].add(value_part)
    attn_out = attended.reshape(tok_rows, 2 * head_width)
    query_grad = qgrad_blocks.reshape(tok_rows, 2 * head_width)
    grad_ext = jnp.stack([key_grad_ext, value_grad_ext])
    owned = group_sum(return_tails(grad_ext, key_reach, tok_rows, hop_count), head_index)
    return (attn_out, query_grad, owned[0], owned[1])


def solution(mesh):
    placed = (P("ctx", "head"), P("ctx", None), P("ctx", None), P("ctx", "head"), P("ctx"))
    return jax.shard_map(
        body,
        mesh=mesh,
        in_specs=placed,
        out_specs=(P("ctx", "head"), P("ctx", "head"), P("ctx", "head"), P("ctx", "head")),
        check_vma=False,
    )
```

profile of v0, /device:TPU:543, one launch (start us, length us, event | category | flops | bytes accessed | tf_op | source)
XLA Modules:
  0.0 73.9 jit_solution(15501444259421066048)
XLA Ops:
  0.7 1.0 %dynamic-slice_bitcast_fusion = (bf16[1,512,128]{2,1,0:T(8,128)(2,1)S(1)}, bf16[1,512,128]{2,1,0:T(8,128)(2,1)S(1)}) fusion(bf16[512,1024]{1,0:T(8,128)(2,1)} %param.23, s32[]{:T(128)S(6)} %select_n.26, bf16[512,1024]{1,0:T(8,128)(2,1)} %param.22), kind=kLoop, calls=%fused_computation.36 | loop fusion | bytes 524292 | tf_op jit(solution)/shard_map/stack | solution.py:53
  1.7 3.7 %collective-permute-start.1 = (bf16[2,512,128]{2,1,0:T(8,128)(2,1)S(1)}, bf16[2,512,128]{2,1,0:T(8,128)(2,1)S(1)}, u32[]{:S(2)}, u32[]{:S(2)}) collective-permute-start(bf16[2,512,128]{2,1,0:T(8,128)(2,1)S(1)} %pad_maximum_fusion.1), channel_id=1, source_target_pairs={{0,32},{32,64},{64,96},{96,128},{128,160},{160,192},{192,224},{224... | collective-permute-start | bytes 786440 | tf_op jit(solution)/shard_map/ppermute | solution.py:13
  5.4 3.1 %collective-permute-start = (bf16[2,512,128]{2,1,0:T(8,128)(2,1)S(1)}, bf16[2,512,128]{2,1,0:T(8,128)(2,1)S(1)}, u32[]{:S(2)}, u32[]{:S(2)}) collective-permute-start(bf16[2,512,128]{2,1,0:T(8,128)(2,1)S(1)} %pad_maximum_fusion.1), channel_id=1, source_target_pairs={{0,64},{32,96},{64,128},{96,160},{128,192},{160,224},{192,256},{22... | collective-permute-start | bytes 786440 | tf_op jit(solution)/shard_map/ppermute | solution.py:13
  8.5 1.1 %copy.12 = bf16[512,256]{0,1:T(8,128)(2,1)S(1)} copy(bf16[512,256]{1,0:T(8,128)(2,1)} %param.24) | data formatting | bytes 524288 | tf_op args[3]
  9.6 1.1 %copy.30 = bf16[512,256]{0,1:T(8,128)(2,1)S(1)} copy(bf16[512,256]{1,0:T(8,128)(2,1)} %param.21) | data formatting | bytes 524288 | tf_op jit(solution)/shard_map/reshape | solution.py:61
  10.7 1.9 %compare_and_fusion = pred[512,1536]{0,1:T(8,128)(4,1)S(1)} fusion(s32[512]{0:T(512)} %param.25, s32[512]{0:T(512)S(1)} %get-tuple-element.99, s32[512]{0:T(512)S(1)} %get-tuple-element.98, s32[1536]{0:T(1024)S(1)} %iota_add_fusion), kind=kLoop, calls=%fused_computation.11 | loop fusion | flops 3932160 | bytes 798720 | tf_op jit(solution)/shard_map/and | solution.py:70
  12.6 3.6 %collective-permute-done = bf16[2,512,128]{2,1,0:T(8,128)(2,1)S(1)} collective-permute-done((bf16[2,512,128]{2,1,0:T(8,128)(2,1)S(1)}, bf16[2,512,128]{2,1,0:T(8,128)(2,1)S(1)}, u32[]{:S(2)}, u32[]{:S(2)}) %collective-permute-start) | collective-permute-done | bytes 262176 | tf_op jit(solution)/shard_map/ppermute | solution.py:13
  16.3 4.9 %fusion.23 = (f32[2,512]{1,0:T(2,128)S(1)}, f32[2,512,1536]{1,2,0:T(8,128)}) fusion(pred[512,1536]{0,1:T(8,128)(4,1)S(1)} %compare_and_fusion, bf16[512,2,128]{0,2,1:T(8,128)(2,1)S(1)} %bitcast.78, bf16[2,1536,128]{2,1,0:T(8,128)(2,1)S(1)} %maximum_maximum_fusion), kind=kOutput, calls=%fused_computation.48 | convolution fusion | flops 410519040 | bytes 8523776 | tf_op jit(solution)/shard_map/sub | solution.py:80
  21.1 3.8 %fusion.7 = bf16[2,512,1536]{1,2,0:T(8,128)(2,1)S(1)} fusion(f32[2,512,1536]{1,2,0:T(8,128)} %get-tuple-element.95, f32[2,512]{1,0:T(2,128)S(1)} %get-tuple-element.94), kind=kLoop, calls=%fused_computation.12 | loop fusion | flops 3145728 | bytes 9441280 | tf_op jit(solution)/shard_map/convert_element_type | solution.py:82
  25.0 1.3 %multiply_reduce_fusion = (f32[512,2]{0,1:T(2,128)S(1)}, bf16[128,2,512]{2,0,1:T(8,128)(2,1)}) fusion(bf16[512,256]{0,1:T(8,128)(2,1)S(1)} %copy.12, bf16[2,512,1536]{1,2,0:T(8,128)(2,1)S(1)} %fusion.7, bf16[2,1536,128]{2,1,0:T(8,128)(2,1)S(1)} %maximum_maximum_fusion), kind=kOutput, calls=%fused_computation.30 | convolution fusion | flops 403307520 | bytes 4067328 | tf_op jit(solution)/shard_map/gqk,kd->qgd/dot_general | solution.py:83
  26.3 1.1 %convolution_bitcast_fusion = f32[1,1536,128]{1,2,0:T(8,128)S(1)} fusion(bf16[2,512,1536]{1,2,0:T(8,128)(2,1)S(1)} %fusion.7, bf16[512,2,128]{0,2,1:T(8,128)(2,1)S(1)} %bitcast.75), kind=kOutput, calls=%fused_computation.13 | convolution fusion | flops 402653184 | bytes 4194304 | tf_op jit(solution)/shard_map/gqk,qgd->kd/dot_general | solution.py:99
  27.5 1.0 %fusion.2 = bf16[2,512,1536]{1,2,0:T(8,128)(2,1)S(1)} fusion(bf16[512,2,128]{0,2,1:T(8,128)(2,1)S(1)} %bitcast.76, f32[2,512]{1,0:T(2,128)S(1)} %bitcast.81, f32[2,512,1536]{1,2,0:T(8,128)S(1)} %bitcast.74, f32[2,512]{1,0:T(2,128)S(1)} %get-tuple-element.94, bf16[2,1536,128]{2,1,0:T(8,128)(2,1)S(1)} %copy-done.3), kind=kOutput, calls=%fused_computation.3 | convolution fusion | flops 408944640 | bytes 10100736 | tf_op jit(solution)/shard_map/qgd,kd->gqk/dot_general | solution.py:86
  28.7 1.1 %fusion.9 = f32[1,1536,128]{1,2,0:T(8,128)S(1)} fusion(bf16[2,512,1536]{1,2,0:T(8,128)(2,1)S(1)} %fusion.2, bf16[512,2,128]{0,2,1:T(8,128)(2,1)S(1)} %bitcast.79), kind=kOutput, calls=%fused_computation.16 | convolution fusion | flops 402849792 | bytes 4194304 | tf_op jit(solution)/shard_map/gqk,qgd->kd/dot_general | solution.py:96
  30.0 2.2 %collective-permute-start.2 = (bf16[2,512,128]{1,2,0:T(8,128)(2,1)S(1)}, bf16[2,512,128]{1,2,0:T(8,128)(2,1)S(1)}, u32[]{:S(2)}, u32[]{:S(2)}) collective-permute-start(bf16[2,512,128]{1,2,0:T(8,128)(2,1)S(1)} %get-tuple-element.90), channel_id=1, source_target_pairs={{64,0},{96,32},{128,64},{160,96},{192,128},{224,160},{256,192},{28... | collective-permute-start | bytes 786440 | tf_op jit(solution)/shard_map/ppermute | solution.py:13
  32.2 2.6 %collective-permute-start.3 = (bf16[2,512,128]{1,2,0:T(8,128)(2,1)S(1)}, bf16[2,512,128]{1,2,0:T(8,128)(2,1)S(1)}, u32[]{:S(2)}, u32[]{:S(2)}) collective-permute-start(bf16[2,512,128]{1,2,0:T(8,128)(2,1)S(1)} %get-tuple-element.91), channel_id=1, source_target_pairs={{32,0},{64,32},{96,64},{128,96},{160,128},{192,160},{224,192},{256... | collective-permute-start | bytes 786440 | tf_op jit(solution)/shard_map/ppermute | solution.py:13
  34.8 4.6 %collective-permute-done.2 = bf16[2,512,128]{1,2,0:T(8,128)(2,1)S(1)} collective-permute-done((bf16[2,512,128]{1,2,0:T(8,128)(2,1)S(1)}, bf16[2,512,128]{1,2,0:T(8,128)(2,1)S(1)}, u32[]{:S(2)}, u32[]{:S(2)}) %collective-permute-start.2) | collective-permute-done | bytes 262176 | tf_op jit(solution)/shard_map/ppermute | solution.py:13
  39.4 3.4 %collective-permute-done.3 = bf16[2,512,128]{1,2,0:T(8,128)(2,1)S(1)} collective-permute-done((bf16[2,512,128]{1,2,0:T(8,128)(2,1)S(1)}, bf16[2,512,128]{1,2,0:T(8,128)(2,1)S(1)}, u32[]{:S(2)}, u32[]{:S(2)}) %collective-permute-start.3) | collective-permute-done | bytes 262176 | tf_op jit(solution)/shard_map/ppermute | solution.py:13
  43.6 2.1 %collective-permute-start.4 = (bf16[2,512,128]{1,2,0:T(8,128)(2,1)}, bf16[2,512,128]{1,2,0:T(8,128)(2,1)}, u32[]{:S(2)}, u32[]{:S(2)}) collective-permute-start(bf16[2,512,128]{1,2,0:T(8,128)(2,1)} %fusion.20), channel_id=1, source_target_pairs={{0,1},{1,0},{2,3},{3,2},{4,5},{5,4},{6,7},{7,6},{8,9},{9,8},{10,11... | collective-permute-start | bytes 786440 | tf_op jit(solution)/shard_map/ppermute | solution.py:17
  45.6 7.3 %collective-permute-done.4 = bf16[2,512,128]{1,2,0:T(8,128)(2,1)} collective-permute-done((bf16[2,512,128]{1,2,0:T(8,128)(2,1)}, bf16[2,512,128]{1,2,0:T(8,128)(2,1)}, u32[]{:S(2)}, u32[]{:S(2)}) %collective-permute-start.4) | collective-permute-done | bytes 262176 | tf_op jit(solution)/shard_map/ppermute | solution.py:17
  53.0 2.2 %fusion.21 = (bf16[2,512,128]{1,2,0:T(8,128)(2,1)}, f32[2,512,128]{1,2,0:T(8,128)}) fusion(bf16[2,512,128]{1,2,0:T(8,128)(2,1)} %collective-permute-done.4, bf16[2,512,128]{1,2,0:T(8,128)(2,1)} %copy-done.5, bf16[2,512,128]{1,2,0:T(8,128)(2,1)S(1)} %collective-permute-done.2, f32[1,1536,128]{1,2,0:T(8,128)} %copy-done, f32[1,1536,128]{1,2,0:T(8,128)} %copy-done.1), kind=kLoop, calls=%fused_computation.46 | loop fusion | flops 1048576 | bytes 3145728 | tf_op jit(solution)/shard_map/convert_element_type | solution.py:39
  55.2 2.1 %collective-permute-start.5 = (bf16[2,512,128]{1,2,0:T(8,128)(2,1)}, bf16[2,512,128]{1,2,0:T(8,128)(2,1)}, u32[]{:S(2)}, u32[]{:S(2)}) collective-permute-start(bf16[2,512,128]{1,2,0:T(8,128)(2,1)} %get-tuple-element.88), channel_id=1, source_target_pairs={{0,2},{1,3},{2,0},{3,1},{4,6},{5,7},{6,4},{7,5},{8,10},{9,11},{10,... | collective-permute-start | bytes 786440 | tf_op jit(solution)/shard_map/ppermute | solution.py:17
  57.4 1.3 %fusion.11 = bf16[128,2,512]{2,0,1:T(8,128)(2,1)} fusion(bf16[2,512,1536]{1,2,0:T(8,128)(2,1)S(1)} %fusion.2, bf16[2,1536,128]{2,1,0:T(8,128)(2,1)S(1)} %copy-done.4), kind=kOutput, calls=%fused_computation.22 | convolution fusion | flops 402915328 | bytes 3801088 | tf_op jit(solution)/shard_map/gqk,kd->qgd/dot_general | solution.py:92
  58.7 1.8 %copy.20 = bf16[512,256]{1,0:T(8,128)(2,1)} copy(bf16[512,256]{0,1:T(8,128)(2,1)} %bitcast.80) | data formatting | bytes 524288
  61.3 11.0 %collective-permute-done.5 = bf16[2,512,128]{1,2,0:T(8,128)(2,1)} collective-permute-done((bf16[2,512,128]{1,2,0:T(8,128)(2,1)}, bf16[2,512,128]{1,2,0:T(8,128)(2,1)}, u32[]{:S(2)}, u32[]{:S(2)}) %collective-permute-start.5) | collective-permute-done | bytes 262176 | tf_op jit(solution)/shard_map/ppermute | solution.py:17
  (34 shorter events, 3.7 us)
Async XLA Ops:
  1.7 10.9 %collective-permute-start.1 = (bf16[2,512,128]{2,1,0:T(8,128)(2,1)S(1)}, bf16[2,512,128]{2,1,0:T(8,128)(2,1)S(1)}, u32[]{:S(2)}, u32[]{:S(2)}) collective-permute-start(bf16[2,512,128]{2,1,0:T(8,128)(2,1)S(1)} %pad_maximum_fusion.1), channel_id=1, source_target_pairs={{0,32},{32,64},{64,96},{96,128},{128,160},{160,192},{192,224},{224... | collective-permute-start | bytes 786440 | tf_op jit(solution)/shard_map/ppermute | solution.py:13
  5.4 10.8 %collective-permute-start = (bf16[2,512,128]{2,1,0:T(8,128)(2,1)S(1)}, bf16[2,512,128]{2,1,0:T(8,128)(2,1)S(1)}, u32[]{:S(2)}, u32[]{:S(2)}) collective-permute-start(bf16[2,512,128]{2,1,0:T(8,128)(2,1)S(1)} %pad_maximum_fusion.1), channel_id=1, source_target_pairs={{0,64},{32,96},{64,128},{96,160},{128,192},{160,224},{192,256},{22... | collective-permute-start | bytes 786440 | tf_op jit(solution)/shard_map/ppermute | solution.py:13
  10.7 10.4 %copy-start.7 = (bf16[512,256]{0,1:T(8,128)(2,1)}, bf16[512,256]{0,1:T(8,128)(2,1)S(1)}, u32[]{:S(2)}) copy-start(bf16[512,256]{0,1:T(8,128)(2,1)S(1)} %copy.30) | copy-start | bytes 786436
  16.2 8.7 %copy-start.2 = (bf16[2,1536,128]{2,1,0:T(8,128)(2,1)}, bf16[2,1536,128]{2,1,0:T(8,128)(2,1)S(1)}, u32[]{:S(2)}) copy-start(bf16[2,1536,128]{2,1,0:T(8,128)(2,1)S(1)} %maximum_maximum_fusion) | copy-start | bytes 2359300
  21.1 6.3 %slice-start = ((s8[6291456]{0:T(1024)(128)(4,1)}), s8[4194304]{0:T(1024)(128)(4,1)S(1)}, s32[]{:S(2)}) async-start(s8[6291456]{0:T(1024)(128)(4,1)} %bitcast.73), calls=%async_computation | async-start | bytes 8388608
  25.0 2.5 %slice-start.1 = ((s8[6291456]{0:T(1024)(128)(4,1)}), s8[2097152]{0:T(1024)(128)(4,1)S(1)}, s32[]{:S(2)}) async-start(s8[6291456]{0:T(1024)(128)(4,1)} %bitcast.73), calls=%async_computation.1 | async-start | bytes 4194304
  26.3 1.2 %copy-start.3 = (bf16[2,1536,128]{2,1,0:T(8,128)(2,1)S(1)}, bf16[2,1536,128]{2,1,0:T(8,128)(2,1)}, u32[]{:S(2)}) copy-start(bf16[2,1536,128]{2,1,0:T(8,128)(2,1)} %copy-done.2) | copy-start | bytes 2359300
  27.5 15.3 %copy-start = (f32[1,1536,128]{1,2,0:T(8,128)}, f32[1,1536,128]{1,2,0:T(8,128)S(1)}, u32[]{:S(2)}) copy-start(f32[1,1536,128]{1,2,0:T(8,128)S(1)} %convolution_bitcast_fusion) | copy-start | bytes 2359300
  27.5 1.2 %copy-start.8 = (bf16[512,256]{0,1:T(8,128)(2,1)S(1)}, bf16[512,256]{0,1:T(8,128)(2,1)}, u32[]{:S(2)}) copy-start(bf16[512,256]{0,1:T(8,128)(2,1)} %copy-done.7) | copy-start | bytes 786436
  29.8 13.7 %copy-start.1 = (f32[1,1536,128]{1,2,0:T(8,128)}, f32[1,1536,128]{1,2,0:T(8,128)S(1)}, u32[]{:S(2)}) copy-start(f32[1,1536,128]{1,2,0:T(8,128)S(1)} %fusion.9) | copy-start | bytes 2359300
  30.0 9.4 %collective-permute-start.2 = (bf16[2,512,128]{1,2,0:T(8,128)(2,1)S(1)}, bf16[2,512,128]{1,2,0:T(8,128)(2,1)S(1)}, u32[]{:S(2)}, u32[]{:S(2)}) collective-permute-start(bf16[2,512,128]{1,2,0:T(8,128)(2,1)S(1)} %get-tuple-element.90), channel_id=1, source_target_pairs={{64,0},{96,32},{128,64},{160,96},{192,128},{224,160},{256,192},{28... | collective-permute-start | bytes 786440 | tf_op jit(solution)/shard_map/ppermute | solution.py:13
  32.2 10.6 %collective-permute-start.3 = (bf16[2,512,128]{1,2,0:T(8,128)(2,1)S(1)}, bf16[2,512,128]{1,2,0:T(8,128)(2,1)S(1)}, u32[]{:S(2)}, u32[]{:S(2)}) collective-permute-start(bf16[2,512,128]{1,2,0:T(8,128)(2,1)S(1)} %get-tuple-element.91), channel_id=1, source_target_pairs={{32,0},{64,32},{96,64},{128,96},{160,128},{192,160},{224,192},{256... | collective-permute-start | bytes 786440 | tf_op jit(solution)/shard_map/ppermute | solution.py:13
  42.7 0.8 %copy-start.5 = (bf16[2,512,128]{1,2,0:T(8,128)(2,1)}, bf16[2,512,128]{1,2,0:T(8,128)(2,1)S(1)}, u32[]{:S(2)}) copy-start(bf16[2,512,128]{1,2,0:T(8,128)(2,1)S(1)} %collective-permute-done.3) | copy-start | bytes 786436
  43.6 9.4 %collective-permute-start.4 = (bf16[2,512,128]{1,2,0:T(8,128)(2,1)}, bf16[2,512,128]{1,2,0:T(8,128)(2,1)}, u32[]{:S(2)}, u32[]{:S(2)}) collective-permute-start(bf16[2,512,128]{1,2,0:T(8,128)(2,1)} %fusion.20), channel_id=1, source_target_pairs={{0,1},{1,0},{2,3},{3,2},{4,5},{5,4},{6,7},{7,6},{8,9},{9,8},{10,11... | collective-permute-start | bytes 786440 | tf_op jit(solution)/shard_map/ppermute | solution.py:17
  45.6 11.7 %copy-start.4 = (bf16[2,1536,128]{2,1,0:T(8,128)(2,1)S(1)}, bf16[2,1536,128]{2,1,0:T(8,128)(2,1)}, u32[]{:S(2)}) copy-start(bf16[2,1536,128]{2,1,0:T(8,128)(2,1)} %copy-done.2) | copy-start | bytes 2359300
  55.2 5.2 %copy-start.6 = (bf16[128,2,512]{2,0,1:T(8,128)(2,1)S(1)}, bf16[128,2,512]{2,0,1:T(8,128)(2,1)}, u32[]{:S(2)}) copy-start(bf16[128,2,512]{2,0,1:T(8,128)(2,1)} %get-tuple-element.97) | copy-start | bytes 786436
  55.2 17.1 %collective-permute-start.5 = (bf16[2,512,128]{1,2,0:T(8,128)(2,1)}, bf16[2,512,128]{1,2,0:T(8,128)(2,1)}, u32[]{:S(2)}, u32[]{:S(2)}) collective-permute-start(bf16[2,512,128]{1,2,0:T(8,128)(2,1)} %get-tuple-element.88), channel_id=1, source_target_pairs={{0,2},{1,3},{2,0},{3,1},{4,6},{5,7},{6,4},{7,5},{8,10},{9,11},{10,... | collective-permute-start | bytes 786440 | tf_op jit(solution)/shard_map/ppermute | solution.py:17
where the time goes:
time: 74.4 us; the launch traced here: 73.9 us
  waiting for transfers between devices  29.9 us (40%)
  starting transfers between devices  15.7 us (21%)
  matrix products  10.8 us (15%)
  other arithmetic  9.88 us (13%)
  local copies, waits for them, and re-layouts  6.73 us (9%)
  between operations  0.93 us (1%)
    ppermute x2, waiting for transfers between devices, from_partner(): lax.ppermute(array, axis, [(i, i ^ 1 << stride) for i in range(lax.axis_s...  18.3 us
    ppermute x4, waiting for transfers between devices, from_behind(): return lax.ppermute(block, axis, route)  11.6 us
    ppermute x4, starting transfers between devices, from_behind(): return lax.ppermute(block, axis, route)  11.5 us
    sub x1, matrix products, body(): weights = jnp.where(visible[None], jnp.exp(masked - row_max), 0.0)  4.86 us
    ppermute x2, starting transfers between devices, from_partner(): lax.ppermute(array, axis, [(i, i ^ 1 << stride) for i in range(lax.axis_s...  4.17 us
    unnamed x25, local copies, waits for them, and re-layouts  3.95 us
    convert_element_type x1, other arithmetic, body(): prob_round = prob_full.astype(jnp.bfloat16)  3.84 us
    convert_element_type x2, other arithmetic, group_sum(): partial_value.astype(jnp.bfloat16)  3.06 us
  transfers between devices with their start and end apart: 6, of which 5 were waited for; matrix products, arithmetic and copies ran while one was open for 11% of the time, Pallas kernels for 0%

commit v1 on v0

v1 whole, which is shorter than its diff:
```python
import math

import jax
import jax.numpy as jnp
from jax import lax
from jax.experimental import pallas as pl
from jax.experimental.pallas import tpu as pltpu
from jax.sharding import PartitionSpec as P

D = 128
WINDOW = 1024
T = 512
H = 256
SCALE = D**-0.5
SCALE2 = SCALE * math.log2(math.e)
MESH = pl.DeviceIdType.MESH
f32, bf16 = jnp.float32, jnp.bfloat16

SEEN = {(0, 0): (0, H), (0, 1): (0, T), (1, 0): (0, T), (1, 1): (0, T), (2, 0): (0, T), (2, 1): (H, T)}


def dot(a, b, ca, cb):
    return lax.dot_general(a, b, (((ca,), (cb,)), ((), ())), preferred_element_type=f32)


def kernel(
    q_hbm, k_hbm, v_hbm, do_hbm, doc_ref,
    o_hbm, dq_hbm, dk_ref, dv_ref,
    q_in, do_in, kv, q2, do2, q_t, do_t, k_t, v_t,
    e_s, dp_s, m_s, l_s, dl_s, o_s,
    own, exch_out, exch_in, g1_out, g0_out, g1_in, g0_in,
    tot, y_out, y_in, o_vm, dq_vm,
    in_sem, out_sem, kv_send, kv_recv, relay_send, ex_send, ex_recv,
    g_send, g1_recv, g0_recv, y_send, y_recv,
):
    ctx = lax.axis_index("ctx")
    head = lax.axis_index("head")
    n_ctx = lax.axis_size("ctx")
    core = lax.rem(ctx, 2)
    even = core == 0
    group = head // 4
    member = lax.rem(head, 4)

    def at(step):
        return (ctx + step, head)

    def peer(j):
        return (ctx, group * 4 + lax.rem(member + j, 4))

    def remote(src, dst, ss, rs, dev):
        return pltpu.make_async_remote_copy(
            src_ref=src, dst_ref=dst, send_sem=ss, recv_sem=rs,
            device_id=dev, device_id_type=MESH,
        )

    cols = pl.ds(pl.multiple_of(group * D, D), D)
    loads = [
        pltpu.make_async_copy(k_hbm.at[:, cols], kv.at[0, 0], in_sem.at[0]),
        pltpu.make_async_copy(v_hbm.at[:, cols], kv.at[0, 1], in_sem.at[1]),
        pltpu.make_async_copy(q_hbm, q_in, in_sem.at[2]),
        pltpu.make_async_copy(do_hbm, do_in, in_sem.at[3]),
    ]
    for c in loads:
        c.start()

    has = {-2: ctx >= 2, -1: ctx >= 1, 1: ctx < n_ctx - 1, 2: ctx < n_ctx - 2}
    barrier = pltpu.get_barrier_semaphore()
    for step in (-1, 1, -2, 2):
        @pl.when(has[step])
        def _(step=step):
            pl.semaphore_signal(barrier, inc=1, device_id=at(step), device_id_type=MESH)
    for j in (1, 2, 3):
        pl.semaphore_signal(barrier, inc=1, device_id=peer(j), device_id_type=MESH)

    loads[0].wait()
    loads[1].wait()
    pl.semaphore_wait(barrier, 3 + sum(has[step].astype(jnp.int32) for step in (-1, 1, -2, 2)))

    def hop1(i):
        return remote(kv.at[0, i], kv.at[1, i], kv_send.at[0, i], kv_recv.at[1, i], at(1))

    def hop2(i):
        return remote(kv.at[0, i], kv.at[2, i], kv_send.at[1, i], kv_recv.at[2, i], at(2))

    def relay(i):
        return remote(kv.at[1, i], kv.at[2, i], relay_send.at[i], kv_recv.at[2, i], at(1))

    def recv2(i):
        return remote(kv.at[0, i], kv.at[2, i], kv_send.at[1, i], kv_recv.at[2, i], at(2))

    for i in (0, 1):
        @pl.when(has[1])
        def _(i=i):
            hop1(i).start()

        @pl.when(even & has[2])
        def _(i=i):
            hop2(i).start()

    @pl.when(ctx == 0)
    def _():
        kv[1] = jnp.zeros_like(kv[1])

    @pl.when(ctx <= 1)
    def _():
        kv[2] = jnp.zeros_like(kv[2])

    loads[2].wait()
    loads[3].wait()
    for half in range(2):
        for h in range(2):
            c = half * T + h * H
            a = q_in[half * H:(half + 1) * H, h * D:(h + 1) * D]
            q2[c:c + H, :] = a
            q_t[:, c:c + H] = a.T
            a = do_in[half * H:(half + 1) * H, h * D:(h + 1) * D]
            do2[c:c + H, :] = a
            do_t[:, c:c + H] = a.T

    doc = doc_ref[0:1, :] - ctx * T

    def forward(b):
        k_t[b] = kv[b, 0].T
        v_t[b] = kv[b, 1].T
        for half in range(2):
            lo_k, hi_k = SEEN[b, half]
            n = hi_k - lo_k
            c0 = half * T
            s = dot(kv[b, 0, lo_k:hi_k, :], q2[c0:c0 + T, :], 1, 1) * SCALE2
            key_pos = lax.broadcasted_iota(jnp.int32, (n, H), 0) + (lo_k - b * T)
            query_pos = lax.broadcasted_iota(jnp.int32, (1, H), 1) + half * H
            first = jnp.maximum(query_pos - (WINDOW - 1), doc[:, half * H:(half + 1) * H])
            visible = key_pos >= first
            if b == 0:
                visible = visible & (key_pos <= query_pos)
            visible = jnp.concatenate([visible, visible], axis=1)
            s = jnp.where(visible, s, -1e30)
            m = jnp.max(s, axis=0, keepdims=True)
            if b > 0:
                m_old = m_s[b - 1, 0:1, c0:c0 + T]
                m = jnp.maximum(m_old, m)
                alpha = jnp.exp2(m_old - m)
            e = jnp.exp2(s - m)
            dp = dot(kv[b, 1, lo_k:hi_k, :], do2[c0:c0 + T, :], 1, 1)
            l = jnp.sum(e, axis=0, keepdims=True)
            dl = jnp.sum(e * dp, axis=0, keepdims=True)
            if b > 0:
                l = l + alpha * l_s[0:1, c0:c0 + T]
                dl = dl + alpha * dl_s[0:1, c0:c0 + T]
            m_s[b, 0:1, c0:c0 + T] = m
            l_s[0:1, c0:c0 + T] = l
            dl_s[0:1, c0:c0 + T] = dl
            eb = e.astype(bf16)
            e_s[b, lo_k:hi_k, c0:c0 + T] = eb
            dp_s[b, lo_k:hi_k, c0:c0 + T] = dp
            o_s[b, :, c0:c0 + T] = dot(v_t[b, :, lo_k:hi_k], eb, 1, 0)

    forward(0)

    for i in (0, 1):
        @pl.when(has[-1])
        def _(i=i):
            hop1(i).wait_recv()

        @pl.when(even & has[-2])
        def _(i=i):
            relay(i).start()

    forward(1)

    for i in (0, 1):
        @pl.when(has[-2])
        def _(i=i):
            recv2(i).wait_recv()

    forward(2)

    l_inv = 1.0 / l_s[0:1, :]
    delta = dl_s[0:1, :] * l_inv
    m = m_s[2, 0:1, :]

    def coef(b):
        return jnp.exp2(m_s[b, 0:1, :] - m) * l_inv

    def assemble(b, parts):
        p0, p1 = parts
        if b == 0:
            return [(0, H, p0 + p1[:H]), (H, T, p1[H:])]
        if b == 1:
            return [(0, T, p0 + p1)]
        return [(0, H, p0[:H]), (H, T, p0[H:] + p1)]

    def value_part(b):
        w = (do_t[...].astype(f32) * coef(b)).astype(bf16)
        parts = []
        for half in range(2):
            lo_k, hi_k = SEEN[b, half]
            c0 = half * T
            parts.append(dot(e_s[b, lo_k:hi_k, c0:c0 + T], w[:, c0:c0 + T], 1, 1))
        return assemble(b, parts)

    dq_acc = [None, None]

    def key_part(b):
        c_b = coef(b)
        w = (q_t[...].astype(f32) * (c_b * SCALE)).astype(bf16)
        parts = []
        for half in range(2):
            lo_k, hi_k = SEEN[b, half]
            c0 = half * T
            ds = e_s[b, lo_k:hi_k, c0:c0 + T].astype(f32)
            ds = (ds * (dp_s[b, lo_k:hi_k, c0:c0 + T] - delta[:, c0:c0 + T])).astype(bf16)
            parts.append(dot(ds, w[:, c0:c0 + T], 1, 1))
            dq = dot(k_t[b, :, lo_k:hi_k], ds, 1, 0) * (c_b[:, c0:c0 + T] * SCALE)
            dq_acc[half] = dq if dq_acc[half] is None else dq_acc[half] + dq
        return assemble(b, parts)

    def exch(i, step):
        return remote(exch_out, exch_in, ex_send, ex_recv, at(step))

    def send_g1(i):
        return remote(g1_out.at[i], g1_in.at[i], g_send.at[0, i], g1_recv.at[i], at(-1))

    def send_g0(i):
        return remote(g0_out.at[i], g0_in.at[i], g_send.at[1, i], g0_recv.at[i], at(-2))

    for a, z, p in value_part(2):
        g0_out[1, a:z, :] = p.astype(bf16)

    @pl.when(jnp.logical_not(even) & has[-2])
    def _():
        exch_out[...] = g0_out[1]
        exch(1, -1).start()

    @pl.when(even & has[-2])
    def _():
        send_g0(1).start()

    for a, z, p in value_part(1):
        own[1, a:z, :] = p

    @pl.when(jnp.logical_not(even))
    def _():
        g1_out[1] = own[1].astype(bf16)
        send_g1(1).start()

    for a, z, p in key_part(2):
        tot[0, a:z, :] = p

    @pl.when(even & has[-2])
    def _():
        g0_out[0] = tot[0].astype(bf16)
        send_g0(0).start()
        exch(1, 1).wait_recv()
        g1_out[1] = (own[1] + exch_in[...].astype(f32)).astype(bf16)
        send_g1(1).start()

    for a, z, p in key_part(1):
        own[0, a:z, :] = p

    @pl.when(jnp.logical_not(even))
    def _():
        g1_out[0] = own[0].astype(bf16)
        send_g1(0).start()

    @pl.when(even & has[-2])
    def _():
        exch_out[...] = own[0].astype(bf16)
        exch(0, 1).start()

    for a, z, p in value_part(0):
        own[1, a:z, :] = p

    @pl.when(jnp.logical_not(even) & has[-2])
    def _():
        exch(0, -1).wait_recv()
        g0_out[0] = (tot[0] + exch_in[...].astype(f32)).astype(bf16)
        send_g0(0).start()

    for a, z, p in key_part(0):
        own[0, a:z, :] = p

    for half in range(2):
        c0 = half * T
        o = None
        for b in range(3):
            part = o_s[b, :, c0:c0 + T] * coef(b)[:, c0:c0 + T]
            o = part if o is None else o + part
        for h in range(2):
            rows, lanes = slice(half * H, (half + 1) * H), slice(h * D, (h + 1) * D)
            o_vm[rows, lanes] = o[:, h * H:(h + 1) * H].T.astype(bf16)
            dq_vm[rows, lanes] = dq_acc[half][:, h * H:(h + 1) * H].T.astype(bf16)
    stores = [
        pltpu.make_async_copy(o_vm, o_hbm, out_sem.at[0]),
        pltpu.make_async_copy(dq_vm, dq_hbm, out_sem.at[1]),
    ]
    for c in stores:
        c.start()

    def y_copy(i, j):
        to = lax.rem(member + j, 4)
        return remote(
            y_out.at[i, pl.ds(pl.multiple_of(to * 32, 32), 32), :], y_in.at[i, j - 1],
            y_send.at[i, j - 1], y_recv.at[i, j - 1], peer(j),
        )

    for i in (1, 0):
        tot[i] = own[i]

        @pl.when(even)
        def _(i=i):
            send_g1(i).wait_recv()
            tot[i] += g1_in[i].astype(f32)

        @pl.when(even & has[2])
        def _(i=i):
            send_g0(i).wait_recv()
            tot[i] += g0_in[i].astype(f32)

        @pl.when(jnp.logical_not(even) & has[1])
        def _(i=i):
            if i == 1:
                send_g1(1).wait_recv()
                tot[1] += g1_in[1].astype(f32)
            else:
                send_g0(0).wait_recv()
                tot[0] += g0_in[0].astype(f32)

        tt = tot[i].T
        own[i] = jnp.concatenate([tt[:, 0:D], tt[:, D:2 * D], tt[:, 2 * D:3 * D], tt[:, 3 * D:]], axis=0)
        y_out[i] = tt.astype(bf16)
        for j in (1, 2, 3):
            y_copy(i, j).start()

    for i, out in ((1, dv_ref), (0, dk_ref)):
        mine = pl.multiple_of(member * 32, 32)
        acc = [own[i, pl.ds(mine + D * c, 32), :] for c in range(4)]
        acc = jnp.concatenate(acc, axis=1)
        for j in (1, 2, 3):
            y_copy(i, j).wait_recv()
            acc = acc + y_in[i, j - 1].astype(f32)
        out[...] = acc

    for i in (0, 1):
        @pl.when(has[1])
        def _(i=i):
            hop1(i).wait_send()

        @pl.when(even & has[2])
        def _(i=i):
            hop2(i).wait_send()

        @pl.when(even & has[-2])
        def _(i=i):
            relay(i).wait_send()
            send_g0(i).wait_send()

        @pl.when(jnp.logical_not(even))
        def _(i=i):
            send_g1(i).wait_send()
        for j in (1, 2, 3):
            y_copy(i, j).wait_send()

    @pl.when(even & has[-2])
    def _():
        send_g1(1).wait_send()
        exch(0, 1).wait_send()

    @pl.when(jnp.logical_not(even) & has[-2])
    def _():
        send_g0(0).wait_send()
        exch(1, -1).wait_send()
    for c in stores:
        c.wait()


def body(queries, keys, values, out_grad, doc_start):
    hbm = pl.BlockSpec(memory_space=pl.ANY)
    vmem = pl.BlockSpec(memory_space=pltpu.VMEM)
    V, DMA = pltpu.VMEM, pltpu.SemaphoreType.DMA
    S = jax.ShapeDtypeStruct
    o, dq, dk, dv = pl.pallas_call(
        kernel,
        out_shape=(S((T, 2 * D), bf16), S((T, 2 * D), bf16), S((32, T), f32), S((32, T), f32)),
        in_specs=[hbm, hbm, hbm, hbm, vmem],
        out_specs=(hbm, hbm, vmem, vmem),
        scratch_shapes=[
            V((T, 2 * D), bf16), V((T, 2 * D), bf16), V((3, 2, T, D), bf16),
            V((2 * T, D), bf16), V((2 * T, D), bf16), V((D, 2 * T), bf16), V((D, 2 * T), bf16),
            V((3, D, T), bf16), V((3, D, T), bf16),
            V((3, T, 2 * T), bf16), V((3, T, 2 * T), f32),
            V((3, 8, 2 * T), f32), V((8, 2 * T), f32), V((8, 2 * T), f32), V((3, D, 2 * T), f32),
            V((2, T, D), f32), V((T, D), bf16), V((T, D), bf16),
            V((2, T, D), bf16), V((2, T, D), bf16), V((2, T, D), bf16), V((2, T, D), bf16),
            V((2, T, D), f32), V((2, D, T), bf16), V((2, 3, 32, T), bf16),
            V((T, 2 * D), bf16), V((T, 2 * D), bf16),
            DMA((4,)), DMA((2,)), DMA((2, 2)), DMA((3, 2)), DMA((2,)), DMA(()), DMA(()),
            DMA((2, 2)), DMA((2,)), DMA((2,)), DMA((2, 3)), DMA((2, 3)),
        ],
        compiler_params=pltpu.CompilerParams(
            collective_id=0, has_side_effects=True, vmem_limit_bytes=56 * 2**20
        ),
    )(queries, keys, values, out_grad, doc_start.reshape(1, T))
    return o, dq, dk.T, dv.T


def solution(mesh):
    placed = (P("ctx", "head"), P("ctx", None), P("ctx", None), P("ctx", "head"), P("ctx"))
    return jax.shard_map(
        body,
        mesh=mesh,
        in_specs=placed,
        out_specs=(P("ctx", "head"),) * 4,
        check_vma=False,
    )
```

time: 74.4 us -> 38.8 us (0.52)
  the two profiles are of different devices: /device:TPU:543 before, /device:TPU:1 now
where the time goes in v1:
time: 38.8 us; the launch traced here: 38.5 us
  Pallas kernels  33.7 us (87%)
  local copies, waits for them, and re-layouts  4.07 us (10%)
  between operations  0.65 us (2%)
    pallas_call x1, Pallas kernels, body(): pl.pallas_call(kernel, out_shape=(S((T, 2 * D), bf16), S((T, 2 * D), bf16...  33.7 us
    unnamed x10, local copies, waits for them, and re-layouts  4.07 us

profile of v1, /device:TPU:1, one launch (start us, length us, event | category | flops | bytes accessed | tf_op | source)
XLA Modules:
  0.0 38.5 jit_solution(6189441514163852279)
XLA Ops:
  0.6 33.7 %shard_map.84 = (bf16[512,256]{1,0:T(8,128)(2,1)}, bf16[512,256]{1,0:T(8,128)(2,1)}, f32[32,512]{1,0:T(8,128)}, f32[32,512]{1,0:T(8,128)}) custom-call(bf16[512,256]{1,0:T(8,128)(2,1)} %q_hbm.1, bf16[512,1024]{1,0:T(8,128)(2,1)} %k_hbm.1, bf16[512,1024]{1,0:T(8,128)(2,1)} %v_hbm.1, bf16[512,256]{1,0:T(8,128)(2,1)} %do_hbm.1, s32[1,512]{1,0:T(1,128)} %bitcast.5), custom_call_target="tpu_custom_call" | custom-call | tf_op jit(solution)/shard_map/pallas_call | solution.py:382
  34.4 0.0 copy-start
  34.4 1.7 %copy.13 = bf16[512,256]{1,0:T(8,128)(2,1)} copy(bf16[512,256]{1,0:T(8,128)(2,1)} %get-tuple-element.16) | data formatting | bytes 524288
  36.1 0.0 copy-done
  36.1 0.0 copy-start.2
  36.1 0.7 %copy.14 = bf16[512,256]{1,0:T(8,128)(2,1)} copy(bf16[512,256]{1,0:T(8,128)(2,1)S(1)} %copy-done) | data formatting | bytes 524288
  36.8 0.2 copy-done.2
  37.0 0.0 copy-start.1
  37.0 0.6 %copy.15 = f32[512,32]{0,1:T(8,128)} copy(f32[512,32]{0,1:T(8,128)S(1)} %bitcast.4) | data formatting | bytes 131072
  37.6 0.2 copy-done.1
  37.8 0.6 %copy.16 = f32[512,32]{0,1:T(8,128)} copy(f32[512,32]{0,1:T(8,128)S(1)} %bitcast.3) | data formatting | bytes 131072
Async XLA Ops:
  34.4 1.7 %copy-start = (bf16[512,256]{1,0:T(8,128)(2,1)S(1)}, bf16[512,256]{1,0:T(8,128)(2,1)}, u32[]{:S(2)}) copy-start(bf16[512,256]{1,0:T(8,128)(2,1)} %get-tuple-element.17) | copy-start | bytes 786436
  36.1 0.9 %copy-start.2 = (f32[32,512]{1,0:T(8,128)S(1)}, f32[32,512]{1,0:T(8,128)}, u32[]{:S(2)}) copy-start(f32[32,512]{1,0:T(8,128)} %get-tuple-element.10) | copy-start | bytes 196612
  37.0 0.9 %copy-start.1 = (f32[32,512]{1,0:T(8,128)S(1)}, f32[32,512]{1,0:T(8,128)}, u32[]{:S(2)}) copy-start(f32[32,512]{1,0:T(8,128)} %get-tuple-element.11) | copy-start | bytes 196612

commit v2 on v1

--- a/solution.py
+++ b/solution.py
@@ -24,13 +24,13 @@
 
 
 def kernel(
-    q_hbm, k_hbm, v_hbm, do_hbm, doc_ref,
-    o_hbm, dq_hbm, dk_ref, dv_ref,
+    q_hbm, k_hbm, v_hbm, do_hbm, doc_hbm,
+    o_vm, dq_vm, dk_ref, dv_ref,
     q_in, do_in, kv, q2, do2, q_t, do_t, k_t, v_t,
-    e_s, dp_s, m_s, l_s, dl_s, o_s,
+    e_s, dp_s, m_s, l_s, dl_s, o_s, doc_ref, o_acc, dq_s,
     own, exch_out, exch_in, g1_out, g0_out, g1_in, g0_in,
-    tot, y_out, y_in, o_vm, dq_vm,
-    in_sem, out_sem, kv_send, kv_recv, relay_send, ex_send, ex_recv,
+    tot, y_out, y_in,
+    in_sem, kv_send, kv_recv, relay_send, ex_send, ex_recv,
     g_send, g1_recv, g0_recv, y_send, y_recv,
 ):
     ctx = lax.axis_index("ctx")
@@ -59,22 +59,30 @@
         pltpu.make_async_copy(v_hbm.at[:, cols], kv.at[0, 1], in_sem.at[1]),
         pltpu.make_async_copy(q_hbm, q_in, in_sem.at[2]),
         pltpu.make_async_copy(do_hbm, do_in, in_sem.at[3]),
+        pltpu.make_async_copy(doc_hbm, doc_ref, in_sem.at[4]),
     ]
     for c in loads:
         c.start()
 
     has = {-2: ctx >= 2, -1: ctx >= 1, 1: ctx < n_ctx - 1, 2: ctx < n_ctx - 2}
     barrier = pltpu.get_barrier_semaphore()
-    for step in (-1, 1, -2, 2):
-        @pl.when(has[step])
-        def _(step=step):
-            pl.semaphore_signal(barrier, inc=1, device_id=at(step), device_id_type=MESH)
     for j in (1, 2, 3):
         pl.semaphore_signal(barrier, inc=1, device_id=peer(j), device_id_type=MESH)
 
+    @pl.when(has[-1])
+    def _():
+        pl.semaphore_signal(barrier, inc=1, device_id=at(-1), device_id_type=MESH)
+
+    @pl.when(even & has[-2])
+    def _():
+        pl.semaphore_signal(barrier, inc=1, device_id=at(-2), device_id_type=MESH)
+
+    dq_s[...] = jnp.zeros_like(dq_s)
+    o_acc[...] = jnp.zeros_like(o_acc)
     loads[0].wait()
     loads[1].wait()
-    pl.semaphore_wait(barrier, 3 + sum(has[step].astype(jnp.int32) for step in (-1, 1, -2, 2)))
+    receivers = has[1].astype(jnp.int32) + (even & has[2]).astype(jnp.int32)
+    pl.semaphore_wait(barrier, 3 + receivers)
 
     def hop1(i):
         return remote(kv.at[0, i], kv.at[1, i], kv_send.at[0, i], kv_recv.at[1, i], at(1))
@@ -97,16 +105,9 @@
         def _(i=i):
             hop2(i).start()
 
-    @pl.when(ctx == 0)
-    def _():
-        kv[1] = jnp.zeros_like(kv[1])
-
-    @pl.when(ctx <= 1)
-    def _():
-        kv[2] = jnp.zeros_like(kv[2])
-
     loads[2].wait()
     loads[3].wait()
+    loads[4].wait()
     for half in range(2):
         for h in range(2):
             c = half * T + h * H
@@ -137,7 +138,7 @@
             s = jnp.where(visible, s, -1e30)
             m = jnp.max(s, axis=0, keepdims=True)
             if b > 0:
-                m_old = m_s[b - 1, 0:1, c0:c0 + T]
+                m_old = m_s[3, 0:1, c0:c0 + T]
                 m = jnp.maximum(m_old, m)
                 alpha = jnp.exp2(m_old - m)
             e = jnp.exp2(s - m)
@@ -148,6 +149,7 @@
                 l = l + alpha * l_s[0:1, c0:c0 + T]
                 dl = dl + alpha * dl_s[0:1, c0:c0 + T]
             m_s[b, 0:1, c0:c0 + T] = m
+            m_s[3, 0:1, c0:c0 + T] = m
             l_s[0:1, c0:c0 + T] = l
             dl_s[0:1, c0:c0 + T] = dl
             eb = e.astype(bf16)
@@ -157,27 +159,25 @@
 
     forward(0)
 
-    for i in (0, 1):
-        @pl.when(has[-1])
-        def _(i=i):
+    @pl.when(has[-1])
+    def _():
+        for i in (0, 1):
             hop1(i).wait_recv()
 
-        @pl.when(even & has[-2])
-        def _(i=i):
-            relay(i).start()
-
-    forward(1)
-
-    for i in (0, 1):
-        @pl.when(has[-2])
-        def _(i=i):
+            @pl.when(even)
+            def _(i=i):
+                relay(i).start()
+        forward(1)
+
+    @pl.when(has[-2])
+    def _():
+        for i in (0, 1):
             recv2(i).wait_recv()
-
-    forward(2)
+        forward(2)
 
     l_inv = 1.0 / l_s[0:1, :]
     delta = dl_s[0:1, :] * l_inv
-    m = m_s[2, 0:1, :]
+    m = m_s[3, 0:1, :]
 
     def coef(b):
         return jnp.exp2(m_s[b, 0:1, :] - m) * l_inv
@@ -198,8 +198,6 @@
             c0 = half * T
             parts.append(dot(e_s[b, lo_k:hi_k, c0:c0 + T], w[:, c0:c0 + T], 1, 1))
         return assemble(b, parts)
-
-    dq_acc = [None, None]
 
     def key_part(b):
         c_b = coef(b)
@@ -212,7 +210,8 @@
             ds = (ds * (dp_s[b, lo_k:hi_k, c0:c0 + T] - delta[:, c0:c0 + T])).astype(bf16)
             parts.append(dot(ds, w[:, c0:c0 + T], 1, 1))
             dq = dot(k_t[b, :, lo_k:hi_k], ds, 1, 0) * (c_b[:, c0:c0 + T] * SCALE)
-            dq_acc[half] = dq if dq_acc[half] is None else dq_acc[half] + dq
+            dq_s[:, c0:c0 + T] += dq
+            o_acc[:, c0:c0 + T] += o_s[b, :, c0:c0 + T] * c_b[:, c0:c0 + T]
         return assemble(b, parts)
 
     def exch(i, step):
@@ -224,49 +223,57 @@
     def send_g0(i):
         return remote(g0_out.at[i], g0_in.at[i], g_send.at[1, i], g0_recv.at[i], at(-2))
 
-    for a, z, p in value_part(2):
-        g0_out[1, a:z, :] = p.astype(bf16)
-
-    @pl.when(jnp.logical_not(even) & has[-2])
-    def _():
-        exch_out[...] = g0_out[1]
-        exch(1, -1).start()
-
-    @pl.when(even & has[-2])
-    def _():
-        send_g0(1).start()
-
-    for a, z, p in value_part(1):
-        own[1, a:z, :] = p
-
-    @pl.when(jnp.logical_not(even))
-    def _():
-        g1_out[1] = own[1].astype(bf16)
-        send_g1(1).start()
-
-    for a, z, p in key_part(2):
-        tot[0, a:z, :] = p
-
-    @pl.when(even & has[-2])
-    def _():
-        g0_out[0] = tot[0].astype(bf16)
-        send_g0(0).start()
-        exch(1, 1).wait_recv()
-        g1_out[1] = (own[1] + exch_in[...].astype(f32)).astype(bf16)
-        send_g1(1).start()
-
-    for a, z, p in key_part(1):
-        own[0, a:z, :] = p
-
-    @pl.when(jnp.logical_not(even))
-    def _():
-        g1_out[0] = own[0].astype(bf16)
-        send_g1(0).start()
-
-    @pl.when(even & has[-2])
-    def _():
-        exch_out[...] = own[0].astype(bf16)
-        exch(0, 1).start()
+    @pl.when(has[-2])
+    def _():
+        for a, z, p in value_part(2):
+            g0_out[1, a:z, :] = p.astype(bf16)
+
+        @pl.when(even)
+        def _():
+            send_g0(1).start()
+
+        @pl.when(jnp.logical_not(even))
+        def _():
+            exch_out[...] = g0_out[1]
+            exch(1, -1).start()
+
+    @pl.when(has[-1])
+    def _():
+        for a, z, p in value_part(1):
+            own[1, a:z, :] = p
+
+        @pl.when(jnp.logical_not(even))
+        def _():
+            g1_out[1] = own[1].astype(bf16)
+            send_g1(1).start()
+
+    @pl.when(has[-2])
+    def _():
+        for a, z, p in key_part(2):
+            tot[0, a:z, :] = p
+
+        @pl.when(even)
+        def _():
+            g0_out[0] = tot[0].astype(bf16)
+            send_g0(0).start()
+            exch(1, 1).wait_recv()
+            g1_out[1] = (own[1] + exch_in[...].astype(f32)).astype(bf16)
+            send_g1(1).start()
+
+    @pl.when(has[-1])
+    def _():
+        for a, z, p in key_part(1):
+            own[0, a:z, :] = p
+
+        @pl.when(even)
+        def _():
+            exch_out[...] = own[0].astype(bf16)
+            exch(0, 1).start()
+
+        @pl.when(jnp.logical_not(even))
+        def _():
+            g1_out[0] = own[0].astype(bf16)
+            send_g1(0).start()
 
     for a, z, p in value_part(0):
         own[1, a:z, :] = p
@@ -281,21 +288,11 @@
         own[0, a:z, :] = p
 
     for half in range(2):
-        c0 = half * T
-        o = None
-        for b in range(3):
-            part = o_s[b, :, c0:c0 + T] * coef(b)[:, c0:c0 + T]
-            o = part if o is None else o + part
         for h in range(2):
+            c = half * T + h * H
             rows, lanes = slice(half * H, (half + 1) * H), slice(h * D, (h + 1) * D)
-            o_vm[rows, lanes] = o[:, h * H:(h + 1) * H].T.astype(bf16)
-            dq_vm[rows, lanes] = dq_acc[half][:, h * H:(h + 1) * H].T.astype(bf16)
-    stores = [
-        pltpu.make_async_copy(o_vm, o_hbm, out_sem.at[0]),
-        pltpu.make_async_copy(dq_vm, dq_hbm, out_sem.at[1]),
-    ]
-    for c in stores:
-        c.start()
+            o_vm[rows, lanes] = o_acc[:, c:c + H].T.astype(bf16)
+            dq_vm[rows, lanes] = dq_s[:, c:c + H].T.astype(bf16)
 
     def y_copy(i, j):
         to = lax.rem(member + j, 4)
@@ -370,37 +367,52 @@
     def _():
         send_g0(0).wait_send()
         exch(1, -1).wait_send()
-    for c in stores:
+
+
+def place(o, dq, dk, dv, o_out, dq_out, dk_out, dv_out, sem):
+    pairs = ((o, o_out), (dq, dq_out), (dk, dk_out), (dv, dv_out))
+    copies = [pltpu.make_async_copy(a, b, sem.at[i]) for i, (a, b) in enumerate(pairs)]
+    for c in copies:
+        c.start()
+    for c in copies:
         c.wait()
 
 
 def body(queries, keys, values, out_grad, doc_start):
-    hbm = pl.BlockSpec(memory_space=pl.ANY)
+    hbm = pl.BlockSpec(memory_space=pltpu.HBM)
     vmem = pl.BlockSpec(memory_space=pltpu.VMEM)
     V, DMA = pltpu.VMEM, pltpu.SemaphoreType.DMA
     S = jax.ShapeDtypeStruct
     o, dq, dk, dv = pl.pallas_call(
         kernel,
         out_shape=(S((T, 2 * D), bf16), S((T, 2 * D), bf16), S((32, T), f32), S((32, T), f32)),
-        in_specs=[hbm, hbm, hbm, hbm, vmem],
-        out_specs=(hbm, hbm, vmem, vmem),
+        in_specs=[hbm] * 5,
+        out_specs=(vmem,)*4,
         scratch_shapes=[
             V((T, 2 * D), bf16), V((T, 2 * D), bf16), V((3, 2, T, D), bf16),
             V((2 * T, D), bf16), V((2 * T, D), bf16), V((D, 2 * T), bf16), V((D, 2 * T), bf16),
             V((3, D, T), bf16), V((3, D, T), bf16),
             V((3, T, 2 * T), bf16), V((3, T, 2 * T), f32),
-            V((3, 8, 2 * T), f32), V((8, 2 * T), f32), V((8, 2 * T), f32), V((3, D, 2 * T), f32),
+            V((4, 8, 2 * T), f32), V((8, 2 * T), f32), V((8, 2 * T), f32), V((3, D, 2 * T), f32),
+            V((1, T), jnp.int32), V((D, 2 * T), f32), V((D, 2 * T), f32),
             V((2, T, D), f32), V((T, D), bf16), V((T, D), bf16),
             V((2, T, D), bf16), V((2, T, D), bf16), V((2, T, D), bf16), V((2, T, D), bf16),
             V((2, T, D), f32), V((2, D, T), bf16), V((2, 3, 32, T), bf16),
-            V((T, 2 * D), bf16), V((T, 2 * D), bf16),
-            DMA((4,)), DMA((2,)), DMA((2, 2)), DMA((3, 2)), DMA((2,)), DMA(()), DMA(()),
+            DMA((5,)), DMA((2, 2)), DMA((3, 2)), DMA((2,)), DMA(()), DMA(()),
             DMA((2, 2)), DMA((2,)), DMA((2,)), DMA((2, 3)), DMA((2, 3)),
         ],
         compiler_params=pltpu.CompilerParams(
-            collective_id=0, has_side_effects=True, vmem_limit_bytes=56 * 2**20
+            collective_id=0, has_side_effects=True, vmem_limit_bytes=int(53.25 * 2**20)
         ),
     )(queries, keys, values, out_grad, doc_start.reshape(1, T))
+    o, dq, dk, dv = pl.pallas_call(
+        place,
+        out_shape=(S((T, 2 * D), bf16), S((T, 2 * D), bf16), S((32, T), f32), S((32, T), f32)),
+        in_specs=[vmem] * 4,
+        out_specs=(hbm,) * 4,
+        scratch_shapes=[DMA((4,))],
+        compiler_params=pltpu.CompilerParams(vmem_limit_bytes=4 * 2**20),
+    )(o, dq, dk, dv)
     return o, dq, dk.T, dv.T
 
 

time: 38.8 us -> 34.7 us (0.89)
  local copies, waits for them, and re-layouts: 4.07 us -> 0.67 us
  Pallas kernels: 33.7 us -> 33.2 us
    unnamed x10 -> x2, local copies, waits for them, and re-layouts: 4.07 us -> 0.67 us
    pallas_call x1, Pallas kernels: 33.7 us -> 32.4 us  [body(): pl.pallas_call(kernel, out_shape=(S((T, 2 * D), bf16), S((T, 2 * D), bf16...]
    pallas_call x0 -> x1, Pallas kernels: none -> 0.86 us  [body(): pl.pallas_call(place, out_shape=(S((T, 2 * D), bf16), S((T, 2 * D), bf16)...]
where the time goes in v2:
time: 34.7 us; the launch traced here: 34.5 us
  Pallas kernels  33.2 us (96%)
  local copies, waits for them, and re-layouts  0.67 us (2%)
  between operations  0.65 us (2%)
    pallas_call x1, Pallas kernels, body(): pl.pallas_call(kernel, out_shape=(S((T, 2 * D), bf16), S((T, 2 * D), bf16...  32.4 us
    pallas_call x1, Pallas kernels, body(): pl.pallas_call(place, out_shape=(S((T, 2 * D), bf16), S((T, 2 * D), bf16)...  0.86 us

profile of v2, /device:TPU:1, one launch (start us, length us, event | category | flops | bytes accessed | tf_op | source)
XLA Modules:
  0.0 34.5 jit_solution(14010317909629138780)
XLA Ops:
  0.6 0.0 copy-start
  0.6 0.7 %copy-done = s32[512]{0:T(512)S(1)} copy-done((s32[512]{0:T(512)S(1)}, s32[512]{0:T(512)}, u32[]{:S(2)}) %copy-start) | copy-done | bytes 2072
  1.3 32.4 %shard_map.84 = (bf16[512,256]{1,0:T(8,128)(2,1)S(1)}, bf16[512,256]{1,0:T(8,128)(2,1)S(1)}, f32[32,512]{1,0:T(8,128)S(1)}, f32[32,512]{1,0:T(8,128)S(1)}) custom-call(bf16[512,256]{1,0:T(8,128)(2,1)} %q_hbm.1, bf16[512,1024]{1,0:T(8,128)(2,1)} %k_hbm.1, bf16[512,1024]{1,0:T(8,128)(2,1)} %v_hbm.1, bf16[512,256]{1,0:T(8,128)(2,1)} %do_hbm.1, s32[1,512]{1,0:T(1,128)S(1)} %bitcast.3), custom_call_target="tpu_custom_call" | custom-call | tf_op jit(solution)/shard_map/pallas_call | solution.py:386
  33.7 0.9 %shard_map.85 = (bf16[512,256]{1,0:T(8,128)(2,1)}, bf16[512,256]{1,0:T(8,128)(2,1)}, f32[32,512]{1,0:T(8,128)}, f32[32,512]{1,0:T(8,128)}) custom-call(bf16[512,256]{1,0:T(8,128)(2,1)S(1)} %get-tuple-element.12.o, bf16[512,256]{1,0:T(8,128)(2,1)S(1)} %get-tuple-element.13.dq, f32[32,512]{1,0:T(8,128)S(1)} %get-tuple-element.14.dk, ...), custom_call_target="tpu_custom_call" | custom-call | tf_op jit(solution)/shard_map/pallas_call | solution.py:408
Async XLA Ops:
  0.6 0.7 %copy-start = (s32[512]{0:T(512)S(1)}, s32[512]{0:T(512)}, u32[]{:S(2)}) copy-start(s32[512]{0:T(512)} %param.9) | copy-start | bytes 6148

commit v3 on v2

v3 whole, which is shorter than its diff:
```python
import math

import jax
import jax.numpy as jnp
from jax import lax
from jax.experimental import pallas as pl
from jax.experimental.pallas import tpu as pltpu
from jax.sharding import PartitionSpec as P

D = 128
WINDOW = 1024
T = 512
H = 256
SCALE = D**-0.5
SCALE2 = SCALE * math.log2(math.e)
MESH = pl.DeviceIdType.MESH
f32, bf16 = jnp.float32, jnp.bfloat16

SEEN = {(0, 0): (0, H), (0, 1): (0, T), (1, 0): (0, T), (1, 1): (0, T), (2, 0): (0, T), (2, 1): (H, T)}


def dot(a, b, ca, cb):
    return lax.dot_general(a, b, (((ca,), (cb,)), ((), ())), preferred_element_type=f32)


PIECES = ((1, 0, T), (0, 0, H), (0, H, T))


def kernel(
    q_hbm, k_hbm, v_hbm, do_hbm, doc_hbm,
    o_vm, dq_vm, dk_ref, dv_ref,
    q_in, do_in, doc_ref, kv, q2, do2, q_t, do_t,
    e_s, dp_s, ds_s, m_s, l_s, dl_s, c_s, delta_s, o_acc, dq_s,
    own, part, exch_out, exch_in, g1_out, g0_out, g1_in, g0_in, y_out, y_in,
    in_sem, kv_send, kv_recv, relay_send, ex_send, ex_recv,
    g1_send, g1_recv, g0_send, g0_recv, y_send, y_recv,
):
    ctx = lax.axis_index("ctx")
    head = lax.axis_index("head")
    n_ctx = lax.axis_size("ctx")
    core = lax.rem(ctx, 2)
    even = core == 0
    odd = core == 1
    group = head // 4
    member = lax.rem(head, 4)

    def at(step):
        return (ctx + step, head)

    def peer(j):
        return (ctx, group * 4 + lax.rem(member + j, 4))

    def remote(src, dst, ss, rs, dev):
        return pltpu.make_async_remote_copy(
            src_ref=src, dst_ref=dst, send_sem=ss, recv_sem=rs,
            device_id=dev, device_id_type=MESH,
        )

    cols = pl.ds(pl.multiple_of(group * D, D), D)
    loads = [
        pltpu.make_async_copy(k_hbm.at[:, cols], kv.at[0, 0], in_sem.at[0]),
        pltpu.make_async_copy(v_hbm.at[:, cols], kv.at[0, 1], in_sem.at[1]),
        pltpu.make_async_copy(q_hbm, q_in, in_sem.at[2]),
        pltpu.make_async_copy(do_hbm, do_in, in_sem.at[3]),
        pltpu.make_async_copy(doc_hbm, doc_ref, in_sem.at[4]),
    ]
    for c in loads:
        c.start()

    has = {-2: ctx >= 2, -1: ctx >= 1, 1: ctx < n_ctx - 1, 2: ctx < n_ctx - 2}
    barrier = pltpu.get_barrier_semaphore()
    for j in (1, 2, 3):
        pl.semaphore_signal(barrier, inc=1, device_id=peer(j), device_id_type=MESH)

    @pl.when(has[-1])
    def _():
        pl.semaphore_signal(barrier, inc=1, device_id=at(-1), device_id_type=MESH)

    @pl.when(even & has[-2])
    def _():
        pl.semaphore_signal(barrier, inc=1, device_id=at(-2), device_id_type=MESH)

    loads[0].wait()
    loads[1].wait()
    receivers = has[1].astype(jnp.int32) + (even & has[2]).astype(jnp.int32)
    pl.semaphore_wait(barrier, 3 + receivers)

    def hop1(i):
        return remote(kv.at[0, i], kv.at[1, i], kv_send.at[0, i], kv_recv.at[1, i], at(1))

    def hop2(i):
        return remote(kv.at[0, i], kv.at[2, i], kv_send.at[1, i], kv_recv.at[2, i], at(2))

    def relay(i):
        return remote(kv.at[1, i], kv.at[2, i], relay_send.at[i], kv_recv.at[2, i], at(1))

    def recv2(i):
        return remote(kv.at[0, i], kv.at[2, i], kv_send.at[1, i], kv_recv.at[2, i], at(2))

    for i in (0, 1):
        @pl.when(has[1])
        def _(i=i):
            hop1(i).start()

        @pl.when(even & has[2])
        def _(i=i):
            hop2(i).start()

    loads[2].wait()
    loads[3].wait()
    loads[4].wait()
    for half in range(2):
        for h in range(2):
            c = half * T + h * H
            a = q_in[half * H:(half + 1) * H, h * D:(h + 1) * D]
            q2[c:c + H, :] = a
            q_t[:, c:c + H] = a.T
            a = do_in[half * H:(half + 1) * H, h * D:(h + 1) * D]
            do2[c:c + H, :] = a
            do_t[:, c:c + H] = a.T

    doc = doc_ref[0:1, :] - ctx * T

    def score(b):
        for half in range(2):
            lo_k, hi_k = SEEN[b, half]
            n = hi_k - lo_k
            c0 = half * T
            s = dot(kv[b, 0, lo_k:hi_k, :], q2[c0:c0 + T, :], 1, 1) * SCALE2
            key_pos = lax.broadcasted_iota(jnp.int32, (n, H), 0) + (lo_k - b * T)
            query_pos = lax.broadcasted_iota(jnp.int32, (1, H), 1) + half * H
            first = jnp.maximum(query_pos - (WINDOW - 1), doc[:, half * H:(half + 1) * H])
            visible = key_pos >= first
            if b == 0:
                visible = visible & (key_pos <= query_pos)
            visible = jnp.concatenate([visible, visible], axis=1)
            s = jnp.where(visible, s, -1e30)
            m = jnp.max(s, axis=0, keepdims=True)
            if b > 0:
                m_old = m_s[3, 0:1, c0:c0 + T]
                m = jnp.maximum(m_old, m)
            e = jnp.exp2(s - m)
            l = jnp.sum(e, axis=0, keepdims=True)
            if b > 0:
                l = l + jnp.exp2(m_old - m) * l_s[0:1, c0:c0 + T]
            m_s[b, 0:1, c0:c0 + T] = m
            m_s[3, 0:1, c0:c0 + T] = m
            l_s[0:1, c0:c0 + T] = l
            e_s[b, lo_k:hi_k, c0:c0 + T] = e.astype(bf16)

    def dprob(b):
        for half in range(2):
            lo_k, hi_k = SEEN[b, half]
            c0 = half * T
            dp = dot(kv[b, 1, lo_k:hi_k, :], do2[c0:c0 + T, :], 1, 1)
            dp_s[b, lo_k:hi_k, c0:c0 + T] = dp
            e = e_s[b, lo_k:hi_k, c0:c0 + T].astype(f32)
            dl = jnp.sum(e * dp, axis=0, keepdims=True)
            if b == 0:
                dl_s[0:1, c0:c0 + T] = dl
            else:
                delta_s[0:1, c0:c0 + T] += dl * c_s[b, 0:1, c0:c0 + T]

    def coef(b):
        c_s[b, 0:1, :] = jnp.exp2(m_s[b, 0:1, :] - m_s[3, 0:1, :]) / l_s[0:1, :]

    def assemble(b, p):
        if b == 0:
            return [(0, H, p[0] + p[1][:, :H]), (H, T, p[1][:, H:])]
        if b == 1:
            return [(0, T, p[0] + p[1])]
        return [(0, H, p[0][:, :H]), (H, T, p[0][:, H:] + p[1])]

    def value_part(b):
        w = (do_t[...].astype(f32) * c_s[b, 0:1, :]).astype(bf16)
        parts = []
        for half in range(2):
            lo_k, hi_k = SEEN[b, half]
            c0 = half * T
            parts.append(dot(w[:, c0:c0 + T], e_s[b, lo_k:hi_k, c0:c0 + T], 1, 1))
        return assemble(b, parts)

    def key_part(b):
        w = (q_t[...].astype(f32) * (c_s[b, 0:1, :] * SCALE)).astype(bf16)
        parts = []
        for half in range(2):
            lo_k, hi_k = SEEN[b, half]
            c0 = half * T
            ds = e_s[b, lo_k:hi_k, c0:c0 + T].astype(f32)
            ds = (ds * (dp_s[b, lo_k:hi_k, c0:c0 + T] - delta_s[0:1, c0:c0 + T])).astype(bf16)
            ds_s[b, lo_k:hi_k, c0:c0 + T] = ds
            parts.append(dot(w[:, c0:c0 + T], ds, 1, 1))
        return assemble(b, parts)

    def row_parts(b):
        k_t, v_t = kv[b, 0].T, kv[b, 1].T
        for half in range(2):
            lo_k, hi_k = SEEN[b, half]
            c0 = half * T
            c = c_s[b, 0:1, c0:c0 + T]
            o = dot(v_t[:, lo_k:hi_k], e_s[b, lo_k:hi_k, c0:c0 + T], 1, 0) * c
            dq = dot(k_t[:, lo_k:hi_k], ds_s[b, lo_k:hi_k, c0:c0 + T], 1, 0) * (c * SCALE)
            if b == 0:
                o_acc[:, c0:c0 + T] = o
                dq_s[:, c0:c0 + T] = dq
            else:
                o_acc[:, c0:c0 + T] += o
                dq_s[:, c0:c0 + T] += dq

    def piece(ref, p):
        i, a, z = PIECES[p]
        return ref.at[i, :, pl.ds(a, z - a)]

    def exch(i, step):
        return remote(exch_out.at[i], exch_in.at[i], ex_send.at[i], ex_recv.at[i], at(step))

    def send_g1(p):
        return remote(piece(g1_out, p), piece(g1_in, p), g1_send.at[p], g1_recv.at[p], at(-1))

    def send_g0(p):
        return remote(piece(g0_out, p), piece(g0_in, p), g0_send.at[p], g0_recv.at[p], at(-2))

    def y_copy(p, j):
        i, a, z = PIECES[p]
        to = pl.multiple_of(lax.rem(member + j, 4) * 32, 32)
        return remote(
            y_out.at[i, pl.ds(to, 32), pl.ds(a, z - a)], y_in.at[i, j - 1, :, pl.ds(a, z - a)],
            y_send.at[p, j - 1], y_recv.at[p, j - 1], peer(j),
        )

    def of(i):
        return [p for p in range(3) if PIECES[p][0] == i]

    def tails(b, i, parts):
        if b == 2:
            for a, z, x in parts:
                g0_out[i, :, a:z] = x.astype(bf16)

            @pl.when(even)
            def _():
                for p in of(i):
                    send_g0(p).start()

            @pl.when(odd)
            def _():
                exch_out[i] = g0_out[i]
                exch(i, -1).start()
        else:
            for a, z, x in parts:
                part[i, :, a:z] = x

            @pl.when(odd)
            def _():
                for p in of(i):
                    _, a, z = PIECES[p]
                    g1_out[i, :, a:z] = part[i, :, a:z].astype(bf16)
                    send_g1(p).start()

    def combine(i):
        exch(i, 1).wait_recv()
        for p in of(i):
            _, a, z = PIECES[p]
            g1_out[i, :, a:z] = (part[i, :, a:z] + exch_in[i, :, a:z].astype(f32)).astype(bf16)
            send_g1(p).start()

    score(0)
    dprob(0)

    @pl.when(has[-1])
    def _():
        hop1(0).wait_recv()

        @pl.when(even)
        def _():
            relay(0).start()
        score(1)

    @pl.when(has[-2])
    def _():
        recv2(0).wait_recv()
        score(2)

    coef(0)
    delta_s[0:1, :] = dl_s[0:1, :] * c_s[0, 0:1, :]

    @pl.when(has[-2])
    def _():
        coef(2)
        tails(2, 1, value_part(2))

    @pl.when(has[-1])
    def _():
        coef(1)
        tails(1, 1, value_part(1))
        hop1(1).wait_recv()

        @pl.when(even)
        def _():
            relay(1).start()
        dprob(1)

    @pl.when(has[-2])
    def _():
        recv2(1).wait_recv()
        dprob(2)

        @pl.when(even)
        def _():
            combine(1)
        tails(2, 0, key_part(2))

    @pl.when(has[-1])
    def _():
        tails(1, 0, key_part(1))

        @pl.when(even)
        def _():
            combine(0)

    for a, z, x in value_part(0):
        own[1, :, a:z] = x
    for a, z, x in key_part(0):
        own[0, :, a:z] = x

    def finish(p):
        i, a, z = PIECES[p]

        @pl.when(has[1])
        def _():
            send_g1(p).wait_recv()
            own[i, :, a:z] += g1_in[i, :, a:z].astype(f32)

        @pl.when(even & has[2])
        def _():
            send_g0(p).wait_recv()
            own[i, :, a:z] += g0_in[i, :, a:z].astype(f32)
        y_out[i, :, a:z] = own[i, :, a:z].astype(bf16)
        for j in (1, 2, 3):
            y_copy(p, j).start()

    finish(0)

    row_parts(0)

    @pl.when(has[-1])
    def _():
        row_parts(1)

    @pl.when(has[-2])
    def _():
        row_parts(2)

    for half in range(2):
        for h in range(2):
            c = half * T + h * H
            rows, lanes = slice(half * H, (half + 1) * H), slice(h * D, (h + 1) * D)
            o_vm[rows, lanes] = o_acc[:, c:c + H].T.astype(bf16)
            dq_vm[rows, lanes] = dq_s[:, c:c + H].T.astype(bf16)

    finish(1)
    finish(2)

    mine = pl.multiple_of(member * 32, 32)
    for p in range(3):
        i, a, z = PIECES[p]
        acc = own[i, pl.ds(mine, 32), a:z]
        for j in (1, 2, 3):
            y_copy(p, j).wait_recv()
            acc = acc + y_in[i, j - 1, :, a:z].astype(f32)
        (dk_ref, dv_ref)[i][:, a:z] = acc

    for i in (0, 1):
        @pl.when(has[1])
        def _(i=i):
            hop1(i).wait_send()

        @pl.when(even & has[2])
        def _(i=i):
            hop2(i).wait_send()

        @pl.when(even & has[-1])
        def _(i=i):
            relay(i).wait_send()

        @pl.when(odd & has[-2])
        def _(i=i):
            exch(i, -1).wait_send()

    for p in range(3):
        @pl.when(has[-1])
        def _(p=p):
            send_g1(p).wait_send()

        @pl.when(even & has[-2])
        def _(p=p):
            send_g0(p).wait_send()
        for j in (1, 2, 3):
            y_copy(p, j).wait_send()


def place(o, dq, dk, dv, o_out, dq_out, dk_out, dv_out, sem):
    pairs = ((o, o_out), (dq, dq_out), (dk, dk_out), (dv, dv_out))
    copies = [pltpu.make_async_copy(a, b, sem.at[i]) for i, (a, b) in enumerate(pairs)]
    for c in copies:
        c.start()
    for c in copies:
        c.wait()


def body(queries, keys, values, out_grad, doc_start):
    hbm = pl.BlockSpec(memory_space=pltpu.HBM)
    vmem = pl.BlockSpec(memory_space=pltpu.VMEM)
    V, DMA = pltpu.VMEM, pltpu.SemaphoreType.DMA
    S = jax.ShapeDtypeStruct
    o, dq, dk, dv = pl.pallas_call(
        kernel,
        out_shape=(S((T, 2 * D), bf16), S((T, 2 * D), bf16), S((32, T), f32), S((32, T), f32)),
        in_specs=[hbm] * 5,
        out_specs=(vmem,)*4,
        scratch_shapes=[
            V((T, 2 * D), bf16), V((T, 2 * D), bf16), V((1, T), jnp.int32), V((3, 2, T, D), bf16),
            V((2 * T, D), bf16), V((2 * T, D), bf16), V((D, 2 * T), bf16), V((D, 2 * T), bf16),
            V((3, T, 2 * T), bf16), V((3, T, 2 * T), f32), V((3, T, 2 * T), bf16),
            V((4, 8, 2 * T), f32), V((8, 2 * T), f32), V((8, 2 * T), f32), V((3, 8, 2 * T), f32),
            V((8, 2 * T), f32), V((D, 2 * T), f32), V((D, 2 * T), f32),
            V((2, D, T), f32), V((2, D, T), f32), V((2, D, T), bf16), V((2, D, T), bf16),
            V((2, D, T), bf16), V((2, D, T), bf16), V((2, D, T), bf16), V((2, D, T), bf16),
            V((2, D, T), bf16), V((2, 3, 32, T), bf16),
            DMA((5,)), DMA((2, 2)), DMA((3, 2)), DMA((2,)), DMA((2,)), DMA((2,)),
            DMA((3,)), DMA((3,)), DMA((3,)), DMA((3,)), DMA((3, 3)), DMA((3, 3)),
        ],
        compiler_params=pltpu.CompilerParams(
            collective_id=0, has_side_effects=True, vmem_limit_bytes=int(53.25 * 2**20)
        ),
    )(queries, keys, values, out_grad, pltpu.with_memory_space_constraint(doc_start.reshape(1, T), pltpu.HBM))
    o, dq, dk, dv = pl.pallas_call(
        place,
        out_shape=(S((T, 2 * D), bf16), S((T, 2 * D), bf16), S((32, T), f32), S((32, T), f32)),
        in_specs=[vmem] * 4,
        out_specs=(hbm,) * 4,
        scratch_shapes=[DMA((4,))],
        compiler_params=pltpu.CompilerParams(vmem_limit_bytes=4 * 2**20),
    )(o, dq, dk, dv)
    return o, dq, dk.T, dv.T


def solution(mesh):
    placed = (P("ctx", "head"), P("ctx", None), P("ctx", None), P("ctx", "head"), P("ctx"))
    return jax.shard_map(
        body,
        mesh=mesh,
        in_specs=placed,
        out_specs=(P("ctx", "head"),) * 4,
        check_vma=False,
    )
```

time: 34.7 us -> 31.6 us (0.911)
  Pallas kernels: 33.2 us -> 30.8 us
  local copies, waits for them, and re-layouts: 0.67 us -> 0 us
    pallas_call x1, Pallas kernels: 32.4 us -> 30 us  [body(): pl.pallas_call(kernel, out_shape=(S((T, 2 * D), bf16), S((T, 2 * D), bf16...]
    unnamed x2 -> x0, local copies, waits for them, and re-layouts: 0.67 us -> none
where the time goes in v3:
time: 31.6 us; the launch traced here: 31.5 us
  Pallas kernels  30.8 us (97%)
  between operations  0.64 us (2%)
    pallas_call x1, Pallas kernels, body(): pl.pallas_call(kernel, out_shape=(S((T, 2 * D), bf16), S((T, 2 * D), bf16...  30 us
    pallas_call x1, Pallas kernels, body(): pl.pallas_call(place, out_shape=(S((T, 2 * D), bf16), S((T, 2 * D), bf16)...  0.86 us

profile of v3, /device:TPU:1, one launch (start us, length us, event | category | flops | bytes accessed | tf_op | source)
XLA Modules:
  0.0 31.5 jit_solution(7060310033625871)
XLA Ops:
  0.6 30.0 %shard_map.84 = (bf16[512,256]{1,0:T(8,128)(2,1)S(1)}, bf16[512,256]{1,0:T(8,128)(2,1)S(1)}, f32[32,512]{1,0:T(8,128)S(1)}, f32[32,512]{1,0:T(8,128)S(1)}) custom-call(bf16[512,256]{1,0:T(8,128)(2,1)} %q_hbm.1, bf16[512,1024]{1,0:T(8,128)(2,1)} %k_hbm.1, bf16[512,1024]{1,0:T(8,128)(2,1)} %v_hbm.1, bf16[512,256]{1,0:T(8,128)(2,1)} %do_hbm.1, s32[1,512]{1,0:T(1,128)} %bitcast.3), custom_call_target="tpu_custom_call" | custom-call | tf_op jit(solution)/shard_map/pallas_call | solution.py:415
  30.6 0.9 %shard_map.85 = (bf16[512,256]{1,0:T(8,128)(2,1)}, bf16[512,256]{1,0:T(8,128)(2,1)}, f32[32,512]{1,0:T(8,128)}, f32[32,512]{1,0:T(8,128)}) custom-call(bf16[512,256]{1,0:T(8,128)(2,1)S(1)} %get-tuple-element.12.o, bf16[512,256]{1,0:T(8,128)(2,1)S(1)} %get-tuple-element.13.dq, f32[32,512]{1,0:T(8,128)S(1)} %get-tuple-element.14.dk, ...), custom_call_target="tpu_custom_call" | custom-call | tf_op jit(solution)/shard_map/pallas_call | solution.py:436

commit v4 on v3

--- a/solution.py
+++ b/solution.py
@@ -33,7 +33,7 @@
     e_s, dp_s, ds_s, m_s, l_s, dl_s, c_s, delta_s, o_acc, dq_s,
     own, part, exch_out, exch_in, g1_out, g0_out, g1_in, g0_in, y_out, y_in,
     in_sem, kv_send, kv_recv, relay_send, ex_send, ex_recv,
-    g1_send, g1_recv, g0_send, g0_recv, y_send, y_recv,
+    g1_send, g1_recv, g0_send, g0_recv, y_send, y_recv, here,
 ):
     ctx = lax.axis_index("ctx")
     head = lax.axis_index("head")
@@ -56,6 +56,7 @@
             device_id=dev, device_id_type=MESH,
         )
 
+    source = (k_hbm, v_hbm)
     cols = pl.ds(pl.multiple_of(group * D, D), D)
     loads = [
         pltpu.make_async_copy(k_hbm.at[:, cols], kv.at[0, 0], in_sem.at[0]),
@@ -69,27 +70,38 @@
 
     has = {-2: ctx >= 2, -1: ctx >= 1, 1: ctx < n_ctx - 1, 2: ctx < n_ctx - 2}
     barrier = pltpu.get_barrier_semaphore()
-    for j in (1, 2, 3):
-        pl.semaphore_signal(barrier, inc=1, device_id=peer(j), device_id_type=MESH)
+    up, down = member < 3, member > 0
+
+    def beside(step):
+        return (ctx, head + step)
+
+    def signal(sem, dev):
+        pl.semaphore_signal(sem, inc=1, device_id=dev, device_id_type=MESH)
 
     @pl.when(has[-1])
     def _():
-        pl.semaphore_signal(barrier, inc=1, device_id=at(-1), device_id_type=MESH)
+        signal(barrier, at(-1))
 
     @pl.when(even & has[-2])
     def _():
-        pl.semaphore_signal(barrier, inc=1, device_id=at(-2), device_id_type=MESH)
-
-    loads[0].wait()
-    loads[1].wait()
-    receivers = has[1].astype(jnp.int32) + (even & has[2]).astype(jnp.int32)
-    pl.semaphore_wait(barrier, 3 + receivers)
+        signal(barrier, at(-2))
+
+    @pl.when(up)
+    def _():
+        signal(barrier, beside(1))
+
+    @pl.when(down)
+    def _():
+        signal(barrier, beside(-1))
+
+    greeters = (has[1], even & has[2], up, down)
+    pl.semaphore_wait(barrier, sum(g.astype(jnp.int32) for g in greeters))
 
     def hop1(i):
-        return remote(kv.at[0, i], kv.at[1, i], kv_send.at[0, i], kv_recv.at[1, i], at(1))
+        return remote(source[i].at[:, cols], kv.at[1, i], kv_send.at[0, i], kv_recv.at[1, i], at(1))
 
     def hop2(i):
-        return remote(kv.at[0, i], kv.at[2, i], kv_send.at[1, i], kv_recv.at[2, i], at(2))
+        return remote(source[i].at[:, cols], kv.at[2, i], kv_send.at[1, i], kv_recv.at[2, i], at(2))
 
     def relay(i):
         return remote(kv.at[1, i], kv.at[2, i], relay_send.at[i], kv_recv.at[2, i], at(1))
@@ -105,10 +117,17 @@
         @pl.when(even & has[2])
         def _(i=i):
             hop2(i).start()
+
+    @pl.when(up & down)
+    def _():
+        signal(here.at[0], beside(-1))
+        signal(here.at[1], beside(1))
 
     loads[2].wait()
     loads[3].wait()
     loads[4].wait()
+    loads[0].wait()
+    loads[1].wait()
     for half in range(2):
         for h in range(2):
             c = half * T + h * H
@@ -156,8 +175,8 @@
             dp_s[b, lo_k:hi_k, c0:c0 + T] = dp
             e = e_s[b, lo_k:hi_k, c0:c0 + T].astype(f32)
             dl = jnp.sum(e * dp, axis=0, keepdims=True)
-            if b == 0:
-                dl_s[0:1, c0:c0 + T] = dl
+            if b < 2:
+                dl_s[b, 0:1, c0:c0 + T] = dl
             else:
                 delta_s[0:1, c0:c0 + T] += dl * c_s[b, 0:1, c0:c0 + T]
 
@@ -268,52 +287,44 @@
 
     @pl.when(has[-1])
     def _():
-        hop1(0).wait_recv()
-
-        @pl.when(even)
-        def _():
-            relay(0).start()
-        score(1)
+        for i in (0, 1):
+            hop1(i).wait_recv()
+
+            @pl.when(even)
+            def _(i=i):
+                relay(i).start()
+            (score, dprob)[i](1)
 
     @pl.when(has[-2])
     def _():
         recv2(0).wait_recv()
         score(2)
-
-    coef(0)
-    delta_s[0:1, :] = dl_s[0:1, :] * c_s[0, 0:1, :]
-
-    @pl.when(has[-2])
-    def _():
         coef(2)
         tails(2, 1, value_part(2))
 
+    coef(0)
+    delta_s[0:1, :] = dl_s[0, 0:1, :] * c_s[0, 0:1, :]
+
     @pl.when(has[-1])
     def _():
         coef(1)
         tails(1, 1, value_part(1))
-        hop1(1).wait_recv()
-
+        delta_s[0:1, :] += dl_s[1, 0:1, :] * c_s[1, 0:1, :]
+
+    @pl.when(has[-2])
+    def _():
         @pl.when(even)
         def _():
-            relay(1).start()
-        dprob(1)
-
-    @pl.when(has[-2])
-    def _():
+            combine(1)
         recv2(1).wait_recv()
         dprob(2)
-
-        @pl.when(even)
-        def _():
-            combine(1)
         tails(2, 0, key_part(2))
 
     @pl.when(has[-1])
     def _():
         tails(1, 0, key_part(1))
 
-        @pl.when(even)
+        @pl.when(even & has[-2])
         def _():
             combine(0)
 
@@ -335,10 +346,26 @@
             send_g0(p).wait_recv()
             own[i, :, a:z] += g0_in[i, :, a:z].astype(f32)
         y_out[i, :, a:z] = own[i, :, a:z].astype(bf16)
-        for j in (1, 2, 3):
-            y_copy(p, j).start()
-
-    finish(0)
+
+        @pl.when(member < 2)
+        def _():
+            for j in (3, 2, 1):
+                y_copy(p, j).start()
+
+        @pl.when(member >= 2)
+        def _():
+            for j in (1, 2, 3):
+                y_copy(p, j).start()
+
+    @pl.when(member == 1)
+    def _():
+        pl.semaphore_wait(here.at[0], 1)
+        signal(here.at[2], beside(-1))
+
+    @pl.when(member == 2)
+    def _():
+        pl.semaphore_wait(here.at[1], 1)
+        signal(here.at[2], beside(1))
 
     row_parts(0)
 
@@ -357,8 +384,18 @@
             o_vm[rows, lanes] = o_acc[:, c:c + H].T.astype(bf16)
             dq_vm[rows, lanes] = dq_s[:, c:c + H].T.astype(bf16)
 
-    finish(1)
-    finish(2)
+    @pl.when(member == 0)
+    def _():
+        pl.semaphore_wait(here.at[0], 1)
+        pl.semaphore_wait(here.at[2], 1)
+
+    @pl.when(member == 3)
+    def _():
+        pl.semaphore_wait(here.at[1], 1)
+        pl.semaphore_wait(here.at[2], 1)
+
+    for p in range(3):
+        finish(p)
 
     mine = pl.multiple_of(member * 32, 32)
     for p in range(3):
@@ -421,13 +458,14 @@
             V((T, 2 * D), bf16), V((T, 2 * D), bf16), V((1, T), jnp.int32), V((3, 2, T, D), bf16),
             V((2 * T, D), bf16), V((2 * T, D), bf16), V((D, 2 * T), bf16), V((D, 2 * T), bf16),
             V((3, T, 2 * T), bf16), V((3, T, 2 * T), f32), V((3, T, 2 * T), bf16),
-            V((4, 8, 2 * T), f32), V((8, 2 * T), f32), V((8, 2 * T), f32), V((3, 8, 2 * T), f32),
+            V((4, 8, 2 * T), f32), V((8, 2 * T), f32), V((2, 8, 2 * T), f32), V((3, 8, 2 * T), f32),
             V((8, 2 * T), f32), V((D, 2 * T), f32), V((D, 2 * T), f32),
             V((2, D, T), f32), V((2, D, T), f32), V((2, D, T), bf16), V((2, D, T), bf16),
             V((2, D, T), bf16), V((2, D, T), bf16), V((2, D, T), bf16), V((2, D, T), bf16),
             V((2, D, T), bf16), V((2, 3, 32, T), bf16),
             DMA((5,)), DMA((2, 2)), DMA((3, 2)), DMA((2,)), DMA((2,)), DMA((2,)),
             DMA((3,)), DMA((3,)), DMA((3,)), DMA((3,)), DMA((3, 3)), DMA((3, 3)),
+            pltpu.SemaphoreType.REGULAR((3,)),
         ],
         compiler_params=pltpu.CompilerParams(
             collective_id=0, has_side_effects=True, vmem_limit_bytes=int(53.25 * 2**20)

time: 31.6 us -> 30.1 us (0.953)
  the two profiles are of different devices: /device:TPU:1 before, /device:TPU:199 now
where the time goes in v4:
time: 30.1 us; the launch traced here: 30 us
  Pallas kernels  29.3 us (97%)
  between operations  0.64 us (2%)
    pallas_call x1, Pallas kernels, body(): pl.pallas_call(kernel, out_shape=(S((T, 2 * D), bf16), S((T, 2 * D), bf16...  28.5 us
    pallas_call x1, Pallas kernels, body(): pl.pallas_call(place, out_shape=(S((T, 2 * D), bf16), S((T, 2 * D), bf16)...  0.86 us

profile of v4, /device:TPU:199, one launch (start us, length us, event | category | flops | bytes accessed | tf_op | source)
XLA Modules:
  0.0 30.0 jit_solution(4683407756493443027)
XLA Ops:
  0.6 28.5 %shard_map.84 = (bf16[512,256]{1,0:T(8,128)(2,1)S(1)}, bf16[512,256]{1,0:T(8,128)(2,1)S(1)}, f32[32,512]{1,0:T(8,128)S(1)}, f32[32,512]{1,0:T(8,128)S(1)}) custom-call(bf16[512,256]{1,0:T(8,128)(2,1)} %q_hbm.1, bf16[512,1024]{1,0:T(8,128)(2,1)} %k_hbm.1, bf16[512,1024]{1,0:T(8,128)(2,1)} %v_hbm.1, bf16[512,256]{1,0:T(8,128)(2,1)} %do_hbm.1, s32[1,512]{1,0:T(1,128)} %bitcast.3), custom_call_target="tpu_custom_call" | custom-call | tf_op jit(solution)/shard_map/pallas_call | solution.py:452
  29.1 0.9 %shard_map.85 = (bf16[512,256]{1,0:T(8,128)(2,1)}, bf16[512,256]{1,0:T(8,128)(2,1)}, f32[32,512]{1,0:T(8,128)}, f32[32,512]{1,0:T(8,128)}) custom-call(bf16[512,256]{1,0:T(8,128)(2,1)S(1)} %get-tuple-element.12.o, bf16[512,256]{1,0:T(8,128)(2,1)S(1)} %get-tuple-element.13.dq, f32[32,512]{1,0:T(8,128)S(1)} %get-tuple-element.14.dk, ...), custom_call_target="tpu_custom_call" | custom-call | tf_op jit(solution)/shard_map/pallas_call | solution.py:474

commit v5 on v4

--- a/solution.py
+++ b/solution.py
@@ -30,7 +30,7 @@
     q_hbm, k_hbm, v_hbm, do_hbm, doc_hbm,
     o_vm, dq_vm, dk_ref, dv_ref,
     q_in, do_in, doc_ref, kv, q2, do2, q_t, do_t,
-    e_s, dp_s, ds_s, m_s, l_s, dl_s, c_s, delta_s, o_acc, dq_s,
+    e_s, dp_s, ds_s, m_s, l_s, c_s, delta_s, o_acc, dq_s,
     own, part, exch_out, exch_in, g1_out, g0_out, g1_in, g0_in, y_out, y_in,
     in_sem, kv_send, kv_recv, relay_send, ex_send, ex_recv,
     g1_send, g1_recv, g0_send, g0_recv, y_send, y_recv, here,
@@ -175,10 +175,11 @@
             dp_s[b, lo_k:hi_k, c0:c0 + T] = dp
             e = e_s[b, lo_k:hi_k, c0:c0 + T].astype(f32)
             dl = jnp.sum(e * dp, axis=0, keepdims=True)
-            if b < 2:
-                dl_s[b, 0:1, c0:c0 + T] = dl
+            dl = dl * c_s[b, 0:1, c0:c0 + T]
+            if b == 0:
+                delta_s[0:1, c0:c0 + T] = dl
             else:
-                delta_s[0:1, c0:c0 + T] += dl * c_s[b, 0:1, c0:c0 + T]
+                delta_s[0:1, c0:c0 + T] += dl
 
     def coef(b):
         c_s[b, 0:1, :] = jnp.exp2(m_s[b, 0:1, :] - m_s[3, 0:1, :]) / l_s[0:1, :]
@@ -283,17 +284,15 @@
             send_g1(p).start()
 
     score(0)
-    dprob(0)
 
     @pl.when(has[-1])
     def _():
-        for i in (0, 1):
-            hop1(i).wait_recv()
-
-            @pl.when(even)
-            def _(i=i):
-                relay(i).start()
-            (score, dprob)[i](1)
+        hop1(0).wait_recv()
+
+        @pl.when(even)
+        def _():
+            relay(0).start()
+        score(1)
 
     @pl.when(has[-2])
     def _():
@@ -302,14 +301,22 @@
         coef(2)
         tails(2, 1, value_part(2))
 
-    coef(0)
-    delta_s[0:1, :] = dl_s[0, 0:1, :] * c_s[0, 0:1, :]
-
     @pl.when(has[-1])
     def _():
         coef(1)
         tails(1, 1, value_part(1))
-        delta_s[0:1, :] += dl_s[1, 0:1, :] * c_s[1, 0:1, :]
+
+    coef(0)
+    dprob(0)
+
+    @pl.when(has[-1])
+    def _():
+        hop1(1).wait_recv()
+
+        @pl.when(even)
+        def _():
+            relay(1).start()
+        dprob(1)
 
     @pl.when(has[-2])
     def _():
@@ -458,7 +465,7 @@
             V((T, 2 * D), bf16), V((T, 2 * D), bf16), V((1, T), jnp.int32), V((3, 2, T, D), bf16),
             V((2 * T, D), bf16), V((2 * T, D), bf16), V((D, 2 * T), bf16), V((D, 2 * T), bf16),
             V((3, T, 2 * T), bf16), V((3, T, 2 * T), f32), V((3, T, 2 * T), bf16),
-            V((4, 8, 2 * T), f32), V((8, 2 * T), f32), V((2, 8, 2 * T), f32), V((3, 8, 2 * T), f32),
+            V((4, 8, 2 * T), f32), V((8, 2 * T), f32), V((3, 8, 2 * T), f32),
             V((8, 2 * T), f32), V((D, 2 * T), f32), V((D, 2 * T), f32),
             V((2, D, T), f32), V((2, D, T), f32), V((2, D, T), bf16), V((2, D, T), bf16),
             V((2, D, T), bf16), V((2, D, T), bf16), V((2, D, T), bf16), V((2, D, T), bf16),

time: 30.1 us -> 29.4 us (0.977)
  the two profiles are of different devices: /device:TPU:199 before, /device:TPU:1 now
where the time goes in v5:
time: 29.4 us; the launch traced here: 29.2 us
  Pallas kernels  28.6 us (97%)
  between operations  0.64 us (2%)
    pallas_call x1, Pallas kernels, body(): pl.pallas_call(kernel, out_shape=(S((T, 2 * D), bf16), S((T, 2 * D), bf16...  27.7 us
    pallas_call x1, Pallas kernels, body(): pl.pallas_call(place, out_shape=(S((T, 2 * D), bf16), S((T, 2 * D), bf16)...  0.86 us

profile of v5, /device:TPU:1, one launch (start us, length us, event | category | flops | bytes accessed | tf_op | source)
XLA Modules:
  0.0 29.2 jit_solution(2840180314113722081)
XLA Ops:
  0.6 27.7 %shard_map.84 = (bf16[512,256]{1,0:T(8,128)(2,1)S(1)}, bf16[512,256]{1,0:T(8,128)(2,1)S(1)}, f32[32,512]{1,0:T(8,128)S(1)}, f32[32,512]{1,0:T(8,128)S(1)}) custom-call(bf16[512,256]{1,0:T(8,128)(2,1)} %q_hbm.1, bf16[512,1024]{1,0:T(8,128)(2,1)} %k_hbm.1, bf16[512,1024]{1,0:T(8,128)(2,1)} %v_hbm.1, bf16[512,256]{1,0:T(8,128)(2,1)} %do_hbm.1, s32[1,512]{1,0:T(1,128)} %bitcast.3), custom_call_target="tpu_custom_call" | custom-call | tf_op jit(solution)/shard_map/pallas_call | solution.py:459
  28.4 0.9 %shard_map.85 = (bf16[512,256]{1,0:T(8,128)(2,1)}, bf16[512,256]{1,0:T(8,128)(2,1)}, f32[32,512]{1,0:T(8,128)}, f32[32,512]{1,0:T(8,128)}) custom-call(bf16[512,256]{1,0:T(8,128)(2,1)S(1)} %get-tuple-element.12.o, bf16[512,256]{1,0:T(8,128)(2,1)S(1)} %get-tuple-element.13.dq, f32[32,512]{1,0:T(8,128)S(1)} %get-tuple-element.14.dk, ...), custom_call_target="tpu_custom_call" | custom-call | tf_op jit(solution)/shard_map/pallas_call | solution.py:481

commit v6 on v5

--- a/solution.py
+++ b/solution.py
@@ -75,6 +75,10 @@
     def beside(step):
         return (ctx, head + step)
 
+    late = (ctx == 0) & (head == 0)
+    stand_in = (ctx == 0) & (head == 1)
+    fed = (head == 0) & (ctx >= 1) & (ctx <= 2)
+
     def signal(sem, dev):
         pl.semaphore_signal(sem, inc=1, device_id=dev, device_id_type=MESH)
 
@@ -86,7 +90,7 @@
     def _():
         signal(barrier, at(-2))
 
-    @pl.when(up)
+    @pl.when(up & jnp.logical_not(late))
     def _():
         signal(barrier, beside(1))
 
@@ -94,7 +98,11 @@
     def _():
         signal(barrier, beside(-1))
 
-    greeters = (has[1], even & has[2], up, down)
+    @pl.when(fed)
+    def _():
+        signal(barrier, (0, 1))
+
+    greeters = (has[1], even & has[2], up, down & jnp.logical_not(stand_in), stand_in, stand_in)
     pl.semaphore_wait(barrier, sum(g.astype(jnp.int32) for g in greeters))
 
     def hop1(i):
@@ -103,6 +111,9 @@
     def hop2(i):
         return remote(source[i].at[:, cols], kv.at[2, i], kv_send.at[1, i], kv_recv.at[2, i], at(2))
 
+    def feed(n, i):
+        return remote(source[i].at[:, cols], kv.at[n, i], kv_send.at[n + 1, i], kv_recv.at[n, i], (n, 0))
+
     def relay(i):
         return remote(kv.at[1, i], kv.at[2, i], relay_send.at[i], kv_recv.at[2, i], at(1))
 
@@ -110,15 +121,26 @@
         return remote(kv.at[0, i], kv.at[2, i], kv_send.at[1, i], kv_recv.at[2, i], at(2))
 
     for i in (0, 1):
-        @pl.when(has[1])
+        @pl.when(has[1] & jnp.logical_not(late))
         def _(i=i):
             hop1(i).start()
 
-        @pl.when(even & has[2])
+        @pl.when(even & has[2] & jnp.logical_not(late))
         def _(i=i):
             hop2(i).start()
 
-    @pl.when(up & down)
+        @pl.when(stand_in)
+        def _(i=i):
+            feed(1, i).start()
+            feed(2, i).start()
+
+    @pl.when(late)
+    def _():
+        signal(here.at[3], at(1))
+        signal(here.at[3], at(2))
+        signal(here.at[3], beside(1))
+
+    @pl.when(up & down & jnp.logical_not(stand_in))
     def _():
         signal(here.at[0], beside(-1))
         signal(here.at[1], beside(1))
@@ -299,11 +321,19 @@
         recv2(0).wait_recv()
         score(2)
         coef(2)
+
+        @pl.when(fed & even)
+        def _():
+            pl.semaphore_wait(here.at[3], 1)
         tails(2, 1, value_part(2))
 
     @pl.when(has[-1])
     def _():
         coef(1)
+
+        @pl.when(fed & odd)
+        def _():
+            pl.semaphore_wait(here.at[3], 1)
         tails(1, 1, value_part(1))
 
     coef(0)
@@ -363,6 +393,12 @@
         def _():
             for j in (1, 2, 3):
                 y_copy(p, j).start()
+
+    @pl.when(stand_in)
+    def _():
+        pl.semaphore_wait(here.at[3], 1)
+        signal(here.at[0], beside(-1))
+        signal(here.at[1], beside(1))
 
     @pl.when(member == 1)
     def _():
@@ -414,13 +450,18 @@
         (dk_ref, dv_ref)[i][:, a:z] = acc
 
     for i in (0, 1):
-        @pl.when(has[1])
+        @pl.when(has[1] & jnp.logical_not(late))
         def _(i=i):
             hop1(i).wait_send()
 
-        @pl.when(even & has[2])
+        @pl.when(even & has[2] & jnp.logical_not(late))
         def _(i=i):
             hop2(i).wait_send()
+
+        @pl.when(stand_in)
+        def _(i=i):
+            feed(1, i).wait_send()
+            feed(2, i).wait_send()
 
         @pl.when(even & has[-1])
         def _(i=i):
@@ -470,9 +511,9 @@
             V((2, D, T), f32), V((2, D, T), f32), V((2, D, T), bf16), V((2, D, T), bf16),
             V((2, D, T), bf16), V((2, D, T), bf16), V((2, D, T), bf16), V((2, D, T), bf16),
             V((2, D, T), bf16), V((2, 3, 32, T), bf16),
-            DMA((5,)), DMA((2, 2)), DMA((3, 2)), DMA((2,)), DMA((2,)), DMA((2,)),
+            DMA((5,)), DMA((4, 2)), DMA((3, 2)), DMA((2,)), DMA((2,)), DMA((2,)),
             DMA((3,)), DMA((3,)), DMA((3,)), DMA((3,)), DMA((3, 3)), DMA((3, 3)),
-            pltpu.SemaphoreType.REGULAR((3,)),
+            pltpu.SemaphoreType.REGULAR((4,)),
         ],
         compiler_params=pltpu.CompilerParams(
             collective_id=0, has_side_effects=True, vmem_limit_bytes=int(53.25 * 2**20)

time: 29.4 us -> 28.1 us (0.956)
  the two profiles are of different devices: /device:TPU:1 before, /device:TPU:197 now
where the time goes in v6:
time: 28.1 us; the launch traced here: 28 us
  Pallas kernels  27.3 us (97%)
  between operations  0.64 us (2%)
    pallas_call x1, Pallas kernels, body(): pl.pallas_call(kernel, out_shape=(S((T, 2 * D), bf16), S((T, 2 * D), bf16...  26.5 us
    pallas_call x1, Pallas kernels, body(): pl.pallas_call(place, out_shape=(S((T, 2 * D), bf16), S((T, 2 * D), bf16)...  0.86 us

profile of v6, /device:TPU:197, one launch (start us, length us, event | category | flops | bytes accessed | tf_op | source)
XLA Modules:
  0.0 28.0 jit_solution(2416949106984024683)
XLA Ops:
  0.6 26.5 %shard_map.84 = (bf16[512,256]{1,0:T(8,128)(2,1)S(1)}, bf16[512,256]{1,0:T(8,128)(2,1)S(1)}, f32[32,512]{1,0:T(8,128)S(1)}, f32[32,512]{1,0:T(8,128)S(1)}) custom-call(bf16[512,256]{1,0:T(8,128)(2,1)} %q_hbm.1, bf16[512,1024]{1,0:T(8,128)(2,1)} %k_hbm.1, bf16[512,1024]{1,0:T(8,128)(2,1)} %v_hbm.1, bf16[512,256]{1,0:T(8,128)(2,1)} %do_hbm.1, s32[1,512]{1,0:T(1,128)} %bitcast.3), custom_call_target="tpu_custom_call" | custom-call | tf_op jit(solution)/shard_map/pallas_call | solution.py:500
  27.1 0.9 %shard_map.85 = (bf16[512,256]{1,0:T(8,128)(2,1)}, bf16[512,256]{1,0:T(8,128)(2,1)}, f32[32,512]{1,0:T(8,128)}, f32[32,512]{1,0:T(8,128)}) custom-call(bf16[512,256]{1,0:T(8,128)(2,1)S(1)} %get-tuple-element.12.o, bf16[512,256]{1,0:T(8,128)(2,1)S(1)} %get-tuple-element.13.dq, f32[32,512]{1,0:T(8,128)S(1)} %get-tuple-element.14.dk, ...), custom_call_target="tpu_custom_call" | custom-call | tf_op jit(solution)/shard_map/pallas_call | solution.py:522
